TPU v7x, 512 devices: a whole 4x8x8 slice. The times are simulated.
512 devices in a mesh: gx: 32 (over z_lo, y, core), gy: 16 (over z_hi, x).
Axes of the slice: x: 4, y: 8, z: 8 (z_hi: 4, z_lo: 2; z = z_hi * 2 + z_lo), core: 2. Of those that a mesh axis runs over, the one named last changes fastest.
Arguments:
- traces: bfloat16 [3, 48, 128, 64, 128], P(None, None, 'gx', 'gy'), may hold values from -6 to 6
- dirichlet: int32 [3, 128, 64, 128], P(None, 'gx', 'gy'), may hold values 0 or 1
- visc_class: int32 [128, 64, 128], P('gx', 'gy'), may hold values from 0 to 3
- viscosity: float32 [4], replicated, may hold values from 0.25 to 4
- coarse_diag: float32 [128, 64, 128], P('gx', 'gy'), may hold values from 2 to 16
- solve_map: bfloat16 [256, 288], replicated, may hold values from -0.375 to 0.375
- flux_map: bfloat16 [288, 256], replicated, may hold values from -0.375 to 0.375
Outputs:
- corrected: bfloat16 [3, 48, 128, 64, 128], P(None, None, 'gx', 'gy')
All inputs are finite; a program needn't handle non-finite values. No bound on the sum of `dirichlet` on one device may be relied on, other than what follows from the above.
Results may differ from a plain program's by a relative error of at most 0.005.
Values may be sent and summed in bfloat16 or wider, within the bound.
A program may use at most 64 MiB of HBM per device.

v0:
```python
import math

import jax
import jax.numpy as jnp
from jax import lax
from jax.sharding import PartitionSpec as P

penalty = 0.5


def from_behind(value, axis, steps):
    count = lax.axis_size(axis)
    leading, last = (max(0, -steps), min(count, count - steps))
    return lax.ppermute(value, axis, [(source, source + steps) for source in range(leading, last)])


def corner_table():
    gll_points = [-1.0, -math.sqrt(0.2), math.sqrt(0.2), 1.0]
    table_rows = []
    for node_s in range(4):
        for node_t in range(4):
            table_row = []
            for high_s in range(2):
                for high_t in range(2):
                    table_row.append(
                        (1.0 + (2 * high_s - 1) * gll_points[node_s])
                        * (1.0 + (2 * high_t - 1) * gll_points[node_t])
                        / 4.0
                    )
            table_rows.append(table_row)
    return jnp.asarray(table_rows, dtype=jnp.float32)


def landing(face_slot, high_s, high_t):
    direction = face_slot // 2
    outward = face_slot % 2
    if direction == 0:
        return (outward, high_s, high_t)
    if direction == 1:
        return (high_s, outward, high_t)
    return (high_s, high_t, outward)


def cell_viscosity(visc_class, viscosity):
    result = jnp.zeros(visc_class.shape, jnp.float32)
    for level in range(viscosity.shape[0]):
        result = result + jnp.where(visc_class == level, viscosity[level], jnp.float32(0.0))
    return result


def lift_depth(piece):
    return jnp.concatenate([jnp.zeros_like(piece[..., :1]), piece[..., :-1]], axis=-1)


def vertex_partials(contrib, weights):
    slots, faces = (contrib.shape[0], contrib.shape[1])
    width_x, width_y, cells_z = (contrib.shape[2], contrib.shape[3], contrib.shape[4])
    split_parts = contrib.reshape(slots, 3, faces // 3, width_x, width_y, cells_z)
    corners = jnp.einsum("fmnxyz,nc->fcmxyz", split_parts, weights, precision=lax.Precision.HIGHEST)
    running = jnp.zeros((3, width_x + 1, width_y + 1, cells_z), jnp.float32)
    for face_slot in range(slots):
        for high_s in range(2):
            for high_t in range(2):
                step_x, step_y, step_z = landing(face_slot, high_s, high_t)
                corner_part = corners[face_slot, 2 * high_s + high_t]
                if step_z:
                    corner_part = lift_depth(corner_part)
                running = running + jnp.pad(
                    corner_part, ((0, 0), (step_x, 1 - step_x), (step_y, 1 - step_y), (0, 0))
                )
    return running


def join_plane(partials, incoming):
    width_x = partials.shape[1] - 1
    return jnp.concatenate([partials[:, :1] + incoming[:, None], partials[:, 1:width_x]], axis=1)


def local(traces, dirichlet, visc_class, viscosity, coarse_diag, solve_map, flux_map):
    weights = corner_table()
    faces = traces.shape[1]
    width_x, width_y, cells_z = (traces.shape[2], traces.shape[3], traces.shape[4])
    keep_mask = (1 - dirichlet).astype(jnp.bfloat16)
    lifted = traces * keep_mask[:, None]
    send_x = jnp.concatenate([lifted[0, :, 0], keep_mask[0, 0][None]], axis=0)
    from_xnext = from_behind(send_x, "gx", -1)
    send_y = jnp.concatenate([lifted[1, :, :, 0], keep_mask[1, :, 0][None]], axis=0)
    from_ynext = from_behind(send_y, "gy", -1)
    x_high = jnp.concatenate([lifted[0, :, 1:], from_xnext[:faces, None]], axis=1)
    y_high = jnp.concatenate([lifted[1, :, :, 1:], from_ynext[:faces, :, None]], axis=2)
    z_high = jnp.concatenate(
        [lifted[2, :, :, :, 1:], jnp.zeros_like(lifted[2, :, :, :, :1])], axis=3
    )
    keep_xhigh = jnp.concatenate([keep_mask[0, 1:], from_xnext[faces][None]], axis=0)
    keep_yhigh = jnp.concatenate([keep_mask[1, :, 1:], from_ynext[faces][:, None]], axis=1)
    keep_zhigh = jnp.concatenate(
        [keep_mask[2, :, :, 1:], jnp.zeros_like(keep_mask[2, :, :, :1])], axis=2
    )
    element_traces = jnp.concatenate(
        [lifted[0], x_high, lifted[1], y_high, lifted[2], z_high], axis=0
    )
    cells = width_x * width_y * cells_z
    flat_traces = element_traces.reshape(6 * faces, cells)
    interior = jnp.dot(solve_map, flat_traces, preferred_element_type=jnp.float32).astype(
        jnp.bfloat16
    )
    flux_term = jnp.dot(
        flux_map, interior, preferred_element_type=jnp.float32
    ) + penalty * flat_traces.astype(jnp.float32)
    visc_here = cell_viscosity(visc_class, viscosity)
    face_keep = jnp.stack(
        [keep_mask[0], keep_xhigh, keep_mask[1], keep_yhigh, keep_mask[2], keep_zhigh]
    ).astype(jnp.float32)
    scaled = (visc_here[None] * face_keep).reshape(6, 1, cells)
    contrib = (flux_term.reshape(6, faces, cells) * scaled).reshape(
        6, faces, width_x, width_y, cells_z
    )
    partials = vertex_partials(contrib, weights)
    high_xplane = contrib[1, :, width_x - 1]
    high_yrow = contrib[3, :, :, width_y - 1]
    package_x = jnp.concatenate(
        [
            high_xplane.reshape(faces * width_y, cells_z),
            partials[:, width_x].reshape(3 * (width_y + 1), cells_z),
        ],
        axis=0,
    )
    arrived_x = from_behind(package_x.astype(jnp.bfloat16), "gx", 1).astype(package_x.dtype)
    from_xprev = arrived_x[: faces * width_y].reshape(faces, width_y, cells_z)
    vertex_xprev = arrived_x[faces * width_y :].reshape(3, width_y + 1, cells_z)
    vertex_mid = join_plane(partials, vertex_xprev)
    package_y = jnp.concatenate(
        [
            high_yrow.reshape(faces * width_x, cells_z),
            vertex_mid[:, :, width_y].reshape(3 * width_x, cells_z),
        ],
        axis=0,
    )
    arrived_y = from_behind(package_y.astype(jnp.bfloat16), "gy", 1).astype(package_y.dtype)
    from_yprev = arrived_y[: faces * width_x].reshape(faces, width_x, cells_z)
    vertex_yprev = arrived_y[faces * width_x :].reshape(3, width_x, cells_z)
    coarse_residual = jnp.concatenate(
        [vertex_mid[:, :, :1] + vertex_yprev[:, :, None], vertex_mid[:, :, 1:width_y]], axis=2
    )
    res_x = contrib[0] + jnp.concatenate(
        [from_xprev[:, None], contrib[1, :, : width_x - 1]], axis=1
    )
    res_y = contrib[2] + jnp.concatenate(
        [from_yprev[:, :, None], contrib[3, :, :, : width_y - 1]], axis=2
    )
    res_z = contrib[4] + lift_depth(contrib[5])
    coarse_fix = coarse_residual / coarse_diag[None]
    from_yrow = from_behind(coarse_fix[:, :, 0], "gy", -1)
    widened = jnp.concatenate([coarse_fix, from_yrow[:, :, None]], axis=2)
    from_xplane = from_behind(widened[:, 0], "gx", -1)
    widened = jnp.concatenate([widened, from_xplane[:, None]], axis=1)
    widened = jnp.concatenate([widened, jnp.zeros_like(widened[..., :1])], axis=3)
    results = []
    for direction, residual in enumerate((res_x, res_y, res_z)):
        picks = []
        for high_s in range(2):
            for high_t in range(2):
                step_x, step_y, step_z = landing(2 * direction, high_s, high_t)
                picks.append(
                    widened[
                        :,
                        step_x : step_x + width_x,
                        step_y : step_y + width_y,
                        step_z : step_z + cells_z,
                    ]
                )
        lifted_fix = jnp.einsum(
            "nc,cmxyz->mnxyz", weights, jnp.stack(picks), precision=lax.Precision.HIGHEST
        ).reshape(faces, width_x, width_y, cells_z)
        results.append(residual + keep_mask[direction].astype(jnp.float32) * lifted_fix)
    return jnp.stack(results).astype(jnp.bfloat16)


def solution(mesh):
    in_specs = (
        P(None, None, "gx", "gy", None),
        P(None, "gx", "gy", None),
        P("gx", "gy", None),
        P(),
        P("gx", "gy", None),
        P(),
        P(),
    )
    out_specs = P(None, None, "gx", "gy", None)
    return jax.shard_map(local, mesh=mesh, in_specs=in_specs, out_specs=out_specs, check_vma=False)
```

profile of v0, /device:TPU:191, one launch (start us, length us, event | category | flops | bytes accessed | tf_op | source)
XLA Modules:
  0.0 73.2 jit_solution(8915324975604929746)
XLA Ops:
  0.0 0.8 %subtract_convert_fusion = bf16[3,4,4,128]{3,2,1,0:T(4,128)(2,1)S(1)} fusion(s32[3,4,4,128]{3,2,1,0:T(4,128)} %param.9), kind=kLoop, calls=%fused_computation.104 | loop fusion | flops 12288 | bytes 36864 | tf_op jit(solution)/shard_map/convert_element_type | solution.py:83
  0.8 1.2 %copy_multiply_fusion.5 = bf16[3,48,4,4,128]{4,1,3,2,0:T(8,128)(2,1)S(1)} fusion(bf16[3,48,4,4,128]{4,3,2,1,0:T(4,128)(2,1)} %param.8, bf16[3,4,4,128]{3,2,1,0:T(4,128)(2,1)S(1)} %subtract_convert_fusion), kind=kLoop, calls=%fused_computation.13 | loop fusion | flops 294912 | bytes 1191936 | tf_op jit(solution)/shard_map/mul | solution.py:84
  2.0 2.6 %collective-permute-start = (bf16[49,4,128]{2,0,1:T(8,128)(2,1)S(1)}, bf16[49,4,128]{2,0,1:T(8,128)(2,1)S(1)}, u32[]{:S(2)}, u32[]{:S(2)}) collective-permute-start(bf16[49,4,128]{2,0,1:T(8,128)(2,1)S(1)} %pad_maximum_fusion.9), channel_id=1, source_target_pairs={{16,0},{32,16},{48,32},{64,48},{80,64},{96,80},{112,96},{128,112},... | collective-permute-start | bytes 150536 | tf_op jit(solution)/shard_map/ppermute | solution.py:14
  4.7 2.5 %collective-permute-start.1 = (bf16[49,4,128]{2,0,1:T(8,128)(2,1)S(1)}, bf16[49,4,128]{2,0,1:T(8,128)(2,1)S(1)}, u32[]{:S(2)}, u32[]{:S(2)}) collective-permute-start(bf16[49,4,128]{2,0,1:T(8,128)(2,1)S(1)} %pad_maximum_fusion.10), channel_id=1, source_target_pairs={{1,0},{2,1},{3,2},{4,3},{5,4},{6,5},{7,6},{8,7},{9,8},{10,9},{11,1... | collective-permute-start | bytes 150536 | tf_op jit(solution)/shard_map/ppermute | solution.py:14
  7.5 0.7 fusion.38
  8.3 0.7 constant_dynamic-update-slice_fusion.5
  9.0 2.5 %select_add_fusion = f32[4,4,128]{2,1,0:T(4,128)S(1)} fusion(s32[4,4,128]{2,1,0:T(4,128)S(1)} %copy-done.4, f32[]{:T(128)} %bitcast.15, f32[]{:T(128)} %bitcast.14, f32[]{:T(128)} %bitcast.13, f32[]{:T(128)} %bitcast.12), kind=kLoop, calls=%fused_computation.108 | loop fusion | flops 22528 | bytes 16400 | tf_op jit(solution)/shard_map/add | solution.py:47
  12.3 1.5 %collective-permute-done.1 = bf16[49,4,128]{2,0,1:T(8,128)(2,1)S(1)} collective-permute-done((bf16[49,4,128]{2,0,1:T(8,128)(2,1)S(1)}, bf16[49,4,128]{2,0,1:T(8,128)(2,1)S(1)}, u32[]{:S(2)}, u32[]{:S(2)}) %collective-permute-start.1) | collective-permute-done | bytes 50208 | tf_op jit(solution)/shard_map/ppermute | solution.py:14
  14.3 0.7 constant_dynamic-update-slice_fusion.4
  15.0 0.7 constant_dynamic-update-slice_fusion.3
  15.7 0.7 constant_dynamic-update-slice_fusion.2
  16.4 0.7 constant_dynamic-update-slice_fusion.1
  17.1 0.7 constant_dynamic-update-slice_fusion
  17.8 3.2 %fusion = f32[288,2048]{1,0:T(8,128)S(1)} fusion(bf16[288,256]{1,0:T(8,128)(2,1)S(1)} %copy-done, bf16[288,2048]{1,0:T(8,128)(2,1)} %constant_dynamic-update-slice_fusion, bf16[256,288]{0,1:T(8,128)(2,1)S(1)} %copy-done.7), kind=kOutput, calls=%fused_computation.1 | convolution fusion | flops 606273536 | bytes 3833856 | tf_op jit(solution)/shard_map/dot_general | solution.py:107
  21.0 2.7 %reshape.242 = f32[6,3,16,4,4,128]{5,4,3,2,1,0:T(4,128)} reshape(f32[288,2048]{1,0:T(8,128)S(1)} %fusion) | data formatting | bytes 4718592 | tf_op jit(solution)/shard_map/reshape | solution.py:115
  23.6 2.6 %reshape.241 = f32[6,48,4,4,128]{4,3,2,1,0:T(4,128)} reshape(f32[288,2048]{1,0:T(8,128)S(1)} %fusion) | data formatting | bytes 4718592 | tf_op jit(solution)/shard_map/reshape | solution.py:115
  26.4 3.6 %fusion.2 = f32[6,4,3,4,4,128]{5,1,4,3,2,0:T(4,128)S(1)} fusion(f32[16,4,1,1,1,1]{0,1,5,4,3,2:T(4,128)S(1)} %copy-done.6, f32[6,3,16,4,4,128]{5,4,3,2,1,0:T(4,128)} %reshape.242, f32[6,4,4,128]{3,2,1,0:T(4,128)S(1)} %bitcast.204), kind=kOutput, calls=%fused_computation.6 | convolution fusion | flops 28901376 | bytes 2998528 | tf_op jit(solution)/shard_map/fmnxyz,nc->fcmxyz/dot_general | solution.py:59
  30.7 3.9 %fusion.33 = (bf16[6,48,4,4,128]{4,3,2,0,1:T(4,128)(2,1)S(1)}, f32[6,48,4,4,128]{4,3,2,0,1:T(4,128)}) fusion(f32[6,4,4,128]{3,2,1,0:T(4,128)S(1)} %bitcast.205, f32[6,48,4,4,128]{4,3,2,1,0:T(4,128)} %reshape.241), kind=kLoop, calls=%fused_computation.123 | loop fusion | flops 1179648 | bytes 5947392 | tf_op jit(solution)/shard_map/convert.18
  34.7 1.0 %copy-done.1 = bf16[6,48,4,4,128]{4,3,2,0,1:T(4,128)(2,1)} copy-done((bf16[6,48,4,4,128]{4,3,2,0,1:T(4,128)(2,1)}, bf16[6,48,4,4,128]{4,3,2,0,1:T(4,128)(2,1)S(1)}, u32[]{:S(2)}) %copy-start.1) | copy-done | bytes 1179672
  35.7 6.6 %collective-permute-start.2 = (bf16[207,128]{1,0:T(8,128)(2,1)S(1)}, bf16[207,128]{1,0:T(8,128)(2,1)S(1)}, u32[]{:S(2)}, u32[]{:S(2)}) collective-permute-start(bf16[207,128]{1,0:T(8,128)(2,1)S(1)} %pad_maximum_fusion.11), channel_id=1, source_target_pairs={{0,16},{16,32},{32,48},{48,64},{64,80},{80,96},{96,112},{112,128},... | collective-permute-start | bytes 158984 | tf_op jit(solution)/shard_map/ppermute | solution.py:14
  42.9 1.0 %slice.428 = bf16[1,48,4,1,128]{4,3,2,0,1:T(2,128)(2,1)S(1)} slice(bf16[6,48,4,4,128]{4,3,2,0,1:T(4,128)(2,1)} %copy-done.1), slice={[3:4], [0:48], [0:4], [3:4], [0:128]} | slice | bytes 98304 | tf_op jit(solution)/shard_map/slice | solution.py:120
  43.9 1.0 %slice.422 = f32[1,48,3,4,128]{4,3,2,0,1:T(4,128)S(1)} slice(f32[6,48,4,4,128]{4,3,2,0,1:T(4,128)} %get-tuple-element.6), slice={[1:2], [0:48], [0:3], [0:4], [0:128]} | slice | bytes 589824 | tf_op jit(solution)/shard_map/slice | solution.py:146
  44.9 1.0 %slice.435 = f32[1,48,4,3,128]{4,3,2,0,1:T(4,128)S(1)} slice(f32[6,48,4,4,128]{4,3,2,0,1:T(4,128)} %get-tuple-element.6), slice={[3:4], [0:48], [0:4], [0:3], [0:128]} | slice | bytes 589824 | tf_op jit(solution)/shard_map/slice | solution.py:149
  47.2 4.4 %collective-permute-start.3 = (bf16[204,128]{1,0:T(8,128)(2,1)S(1)}, bf16[204,128]{1,0:T(8,128)(2,1)S(1)}, u32[]{:S(2)}, u32[]{:S(2)}) collective-permute-start(bf16[204,128]{1,0:T(8,128)(2,1)S(1)} %pad_maximum_fusion.12), channel_id=1, source_target_pairs={{0,1},{1,2},{2,3},{3,4},{4,5},{5,6},{6,7},{7,8},{8,9},{9,10},{10,1... | collective-permute-start | bytes 156680 | tf_op jit(solution)/shard_map/ppermute | solution.py:14
  51.6 1.2 %collective-permute-done.3 = bf16[204,128]{1,0:T(8,128)(2,1)S(1)} collective-permute-done((bf16[204,128]{1,0:T(8,128)(2,1)S(1)}, bf16[204,128]{1,0:T(8,128)(2,1)S(1)}, u32[]{:S(2)}, u32[]{:S(2)}) %collective-permute-start.3) | collective-permute-done | bytes 52256 | tf_op jit(solution)/shard_map/ppermute | solution.py:14
  52.9 1.9 %collective-permute-start.4 = (f32[3,4,128]{2,1,0:T(4,128)S(1)}, f32[3,4,128]{2,1,0:T(4,128)S(1)}, u32[]{:S(2)}, u32[]{:S(2)}) collective-permute-start(f32[3,4,128]{2,1,0:T(4,128)S(1)} %bitcast.244), channel_id=1, source_target_pairs={{1,0},{2,1},{3,2},{4,3},{5,4},{6,5},{7,6},{8,7},{9,8},{10,9},{11,1... | collective-permute-start | bytes 18440 | tf_op jit(solution)/shard_map/ppermute | solution.py:14
  54.8 6.9 %collective-permute-done.4 = f32[3,4,128]{2,1,0:T(4,128)S(1)} collective-permute-done((f32[3,4,128]{2,1,0:T(4,128)S(1)}, f32[3,4,128]{2,1,0:T(4,128)S(1)}, u32[]{:S(2)}, u32[]{:S(2)}) %collective-permute-start.4) | collective-permute-done | bytes 6176 | tf_op jit(solution)/shard_map/ppermute | solution.py:14
  61.8 2.1 %collective-permute-start.5 = (f32[3,5,128]{2,1,0:T(8,128)S(1)}, f32[3,5,128]{2,1,0:T(8,128)S(1)}, u32[]{:S(2)}, u32[]{:S(2)}) collective-permute-start(f32[3,5,128]{2,1,0:T(8,128)S(1)} %maximum_bitcast_fusion), channel_id=1, source_target_pairs={{16,0},{32,16},{48,32},{64,48},{80,64},{96,80},{112,96},{128,112},... | collective-permute-start | bytes 23048 | tf_op jit(solution)/shard_map/ppermute | solution.py:14
  63.9 5.0 %collective-permute-done.5 = f32[3,5,128]{2,1,0:T(8,128)S(1)} collective-permute-done((f32[3,5,128]{2,1,0:T(8,128)S(1)}, f32[3,5,128]{2,1,0:T(8,128)S(1)}, u32[]{:S(2)}, u32[]{:S(2)}) %collective-permute-start.5) | collective-permute-done | bytes 7712 | tf_op jit(solution)/shard_map/ppermute | solution.py:14
  69.7 0.5 convolution_bitcast_fusion.2
  71.1 0.6 fusion.5
  72.1 1.0 %copy.159 = bf16[3,48,4,4,128]{4,3,2,1,0:T(4,128)(2,1)} copy(bf16[3,48,4,4,128]{4,3,2,0,1:T(4,128)(2,1)S(1)} %pad_maximum_fusion) | data formatting | bytes 1179648 | tf_op jit(solution)/shard_map/stack | solution.py:176
  (112 shorter events, 6.4 us)
Async XLA Ops:
  0.0 17.8 %copy-start = (bf16[288,256]{1,0:T(8,128)(2,1)S(1)}, bf16[288,256]{1,0:T(8,128)(2,1)}, u32[]{:S(2)}) copy-start(bf16[288,256]{1,0:T(8,128)(2,1)} %param.14) | copy-start | bytes 442372
  0.0 7.5 %copy-start.5 = (f32[4]{0:T(128)S(1)}, f32[4]{0:T(128)}, u32[]{:S(2)}) copy-start(f32[4]{0:T(128)} %param.11) | copy-start | bytes 52
  2.0 7.0 %copy-start.4 = (s32[4,4,128]{2,1,0:T(4,128)S(1)}, s32[4,4,128]{2,1,0:T(4,128)}, u32[]{:S(2)}) copy-start(s32[4,4,128]{2,1,0:T(4,128)} %param.10) | copy-start | bytes 24580
  2.0 12.0 %collective-permute-start = (bf16[49,4,128]{2,0,1:T(8,128)(2,1)S(1)}, bf16[49,4,128]{2,0,1:T(8,128)(2,1)S(1)}, u32[]{:S(2)}, u32[]{:S(2)}) collective-permute-start(bf16[49,4,128]{2,0,1:T(8,128)(2,1)S(1)} %pad_maximum_fusion.9), channel_id=1, source_target_pairs={{16,0},{32,16},{48,32},{64,48},{80,64},{96,80},{112,96},{128,112},... | collective-permute-start | bytes 150536 | tf_op jit(solution)/shard_map/ppermute | solution.py:14
  4.7 9.1 %collective-permute-start.1 = (bf16[49,4,128]{2,0,1:T(8,128)(2,1)S(1)}, bf16[49,4,128]{2,0,1:T(8,128)(2,1)S(1)}, u32[]{:S(2)}, u32[]{:S(2)}) collective-permute-start(bf16[49,4,128]{2,0,1:T(8,128)(2,1)S(1)} %pad_maximum_fusion.10), channel_id=1, source_target_pairs={{1,0},{2,1},{3,2},{4,3},{5,4},{6,5},{7,6},{8,7},{9,8},{10,9},{11,1... | collective-permute-start | bytes 150536 | tf_op jit(solution)/shard_map/ppermute | solution.py:14
  13.8 4.0 %copy-start.7 = (bf16[256,288]{0,1:T(8,128)(2,1)S(1)}, bf16[256,288]{0,1:T(8,128)(2,1)}, u32[]{:S(2)}) copy-start(bf16[256,288]{0,1:T(8,128)(2,1)} %param.13) | copy-start | bytes 442372
  23.6 2.8 %copy-start.6 = (f32[16,4,1,1,1,1]{0,1,5,4,3,2:T(4,128)S(1)}, f32[16,4,1,1,1,1]{0,1,5,4,3,2:T(4,128)}, u32[]{:S(2)}) copy-start(f32[16,4,1,1,1,1]{0,1,5,4,3,2:T(4,128)} %constant.108) | copy-start | bytes 772
  34.7 1.0 %copy-start.1 = (bf16[6,48,4,4,128]{4,3,2,0,1:T(4,128)(2,1)}, bf16[6,48,4,4,128]{4,3,2,0,1:T(4,128)(2,1)S(1)}, u32[]{:S(2)}) copy-start(bf16[6,48,4,4,128]{4,3,2,0,1:T(4,128)(2,1)S(1)} %get-tuple-element.5) | copy-start | bytes 3538948
  35.7 11.4 %collective-permute-start.2 = (bf16[207,128]{1,0:T(8,128)(2,1)S(1)}, bf16[207,128]{1,0:T(8,128)(2,1)S(1)}, u32[]{:S(2)}, u32[]{:S(2)}) collective-permute-start(bf16[207,128]{1,0:T(8,128)(2,1)S(1)} %pad_maximum_fusion.11), channel_id=1, source_target_pairs={{0,16},{16,32},{32,48},{48,64},{64,80},{80,96},{96,112},{112,128},... | collective-permute-start | bytes 158984 | tf_op jit(solution)/shard_map/ppermute | solution.py:14
  46.0 6.9 %copy-start.2 = (f32[4,4,128]{2,1,0:T(4,128)S(1)}, f32[4,4,128]{2,1,0:T(4,128)}, u32[]{:S(2)}) copy-start(f32[4,4,128]{2,1,0:T(4,128)} %param.12) | copy-start | bytes 24580
  46.2 22.9 %copy-start.3 = (f32[16,4,1,1,1]{0,1,4,3,2:T(4,128)S(1)}, f32[16,4,1,1,1]{0,1,4,3,2:T(4,128)}, u32[]{:S(2)}) copy-start(f32[16,4,1,1,1]{0,1,4,3,2:T(4,128)} %constant.109) | copy-start | bytes 772
  47.2 5.6 %collective-permute-start.3 = (bf16[204,128]{1,0:T(8,128)(2,1)S(1)}, bf16[204,128]{1,0:T(8,128)(2,1)S(1)}, u32[]{:S(2)}, u32[]{:S(2)}) collective-permute-start(bf16[204,128]{1,0:T(8,128)(2,1)S(1)} %pad_maximum_fusion.12), channel_id=1, source_target_pairs={{0,1},{1,2},{2,3},{3,4},{4,5},{5,6},{6,7},{7,8},{8,9},{9,10},{10,1... | collective-permute-start | bytes 156680 | tf_op jit(solution)/shard_map/ppermute | solution.py:14
  52.9 8.9 %collective-permute-start.4 = (f32[3,4,128]{2,1,0:T(4,128)S(1)}, f32[3,4,128]{2,1,0:T(4,128)S(1)}, u32[]{:S(2)}, u32[]{:S(2)}) collective-permute-start(f32[3,4,128]{2,1,0:T(4,128)S(1)} %bitcast.244), channel_id=1, source_target_pairs={{1,0},{2,1},{3,2},{4,3},{5,4},{6,5},{7,6},{8,7},{9,8},{10,9},{11,1... | collective-permute-start | bytes 18440 | tf_op jit(solution)/shard_map/ppermute | solution.py:14
  61.8 7.1 %collective-permute-start.5 = (f32[3,5,128]{2,1,0:T(8,128)S(1)}, f32[3,5,128]{2,1,0:T(8,128)S(1)}, u32[]{:S(2)}, u32[]{:S(2)}) collective-permute-start(f32[3,5,128]{2,1,0:T(8,128)S(1)} %maximum_bitcast_fusion), channel_id=1, source_target_pairs={{16,0},{32,16},{48,32},{64,48},{80,64},{96,80},{112,96},{128,112},... | collective-permute-start | bytes 23048 | tf_op jit(solution)/shard_map/ppermute | solution.py:14
where the time goes:
time: 73.7 us; the launch traced here: 73.2 us
  starting transfers between devices  20 us (27%)
  local copies, waits for them, and re-layouts  19 us (26%)
  waiting for transfers between devices  14.6 us (20%)
  other arithmetic  10.6 us (14%)
  matrix products  8.27 us (11%)
    ppermute x6, starting transfers between devices, from_behind(): lax.ppermute(value, axis, [(source, source + steps) for source in range(l...  20 us
    ppermute x6, waiting for transfers between devices, from_behind(): lax.ppermute(value, axis, [(source, source + steps) for source in range(l...  14.6 us
    reshape x2, local copies, waits for them, and re-layouts, local(): flux_term.reshape(6, faces, cells) * scaled  5.28 us
    unnamed x25, local copies, waits for them, and re-layouts  4.64 us
    another operation x2, other arithmetic  4.57 us
    dot_general x1, matrix products, vertex_partials(): jnp.einsum('fmnxyz,nc->fcmxyz', split_parts, weights, precision=lax.Preci...  3.58 us
    dot_general x1, matrix products, local(): jnp.dot(flux_map, interior, preferred_element_type=jnp.float32)  3.15 us
    add x1, other arithmetic, cell_viscosity(): result + jnp.where(visc_class == level, viscosity[level], jnp.float32(0.0))  2.45 us
  transfers between devices with their start and end apart: 6, of which 4 were waited for; matrix products, arithmetic and copies ran while one was open for 14% of the time, Pallas kernels for 0%

commit v1 on v0

v1 whole, which is shorter than its diff:
```python
import functools
import itertools
import math

import jax
import jax.numpy as jnp
import ml_dtypes
import numpy as np
from jax import lax
from jax.experimental import pallas as pl
from jax.experimental.pallas import tpu as pltpu
from jax.sharding import PartitionSpec as P

MESH = pl.DeviceIdType.MESH
penalty = 0.5
CORNER = 4


def corner_table():
    points = [-1.0, -math.sqrt(0.2), math.sqrt(0.2), 1.0]
    table = np.zeros((16, 4), np.float64)
    for a, b, p, q in itertools.product(range(4), range(4), range(2), range(2)):
        table[4 * a + b, 2 * p + q] = (1 + (2 * p - 1) * points[a]) * (1 + (2 * q - 1) * points[b]) / 4
    return table.astype(np.float32)


def in_two(table):
    high = table.astype(ml_dtypes.bfloat16)
    low = (table - high.astype(np.float32)).astype(ml_dtypes.bfloat16)
    return high, low


def gather_table():
    weights = corner_table()
    table = np.zeros((32, 6, 3, 16), np.float32)
    for dx, dy, dz, m in itertools.product(range(2), range(2), range(2), range(3)):
        row = 16 * dx + 8 * dy + CORNER * dz + m
        table[row, dx, m] = weights[:, 2 * dy + dz]
        table[row, 2 + dy, m] = weights[:, 2 * dx + dz]
        table[row, 4 + dz, m] = weights[:, 2 * dx + dy]
    return np.concatenate(in_two(table.reshape(32, 288)), axis=0)


def spread_table():
    weights = corner_table()
    table = np.zeros((3, 3, 16, 32), np.float32)
    for dx, dy, dz, m in itertools.product(range(2), range(2), range(2), range(3)):
        column = 16 * dx + 8 * dy + CORNER * dz + m
        if dx == 0:
            table[0, m, :, column] = weights[:, 2 * dy + dz]
        if dy == 0:
            table[1, m, :, column] = weights[:, 2 * dx + dz]
        if dz == 0:
            table[2, m, :, column] = weights[:, 2 * dx + dy]
    high, low = in_two(table.reshape(144, 32))
    return np.concatenate([high, high, low], axis=1)


def kernel(
    count_x, count_y,
    lifted, keep, visc, diag, solve_t, flux_map, gather, spread,
    out,
    halo_x, halo_y, keep_x, keep_y, residual, high, send_x, send_y, recv_x, recv_y, vertex, rim_x, rim_y, rim_c,
    send_sem, recv_sem,
):
    wx, wy = lifted.shape[1], lifted.shape[2]
    faces, depth = lifted.shape[3], lifted.shape[4]
    me_x, me_y = lax.axis_index("gx"), lax.axis_index("gy")
    there = {-1: (me_x > 0, me_y > 0), 0: (None, None), 1: (me_x < count_x - 1, me_y < count_y - 1)}

    def present(dx, dy):
        a, b = there[dx][0], there[dy][1]
        if a is None:
            return b
        return a if b is None else jnp.logical_and(a, b)

    def device(dx, dy):
        return {"gx": me_x + dx, "gy": me_y + dy}

    around = [(dx, dy) for dx in (-1, 0, 1) for dy in (-1, 0, 1) if (dx, dy) != (0, 0)]
    barrier = pltpu.get_barrier_semaphore()
    total = 0
    for dx, dy in around:
        here = present(dx, dy)
        total = total + here.astype(jnp.int32)

        @pl.when(here)
        def _():
            pl.semaphore_signal(barrier, inc=1, device_id=device(dx, dy), device_id_type=MESH)

    pl.semaphore_wait(barrier, total)

    class Exchange:
        def __init__(self, slot, dx, dy, source, target):
            self.to, self.origin, self.target = present(dx, dy), present(-dx, -dy), target
            self.copy = pltpu.make_async_remote_copy(
                src_ref=source, dst_ref=target, send_sem=send_sem.at[slot], recv_sem=recv_sem.at[slot],
                device_id=device(dx, dy), device_id_type=MESH,
            )

        def start(self):
            pl.when(self.to)(self.copy.start)

            @pl.when(jnp.logical_not(self.origin))
            def _():
                self.target[...] = jnp.zeros(self.target.shape, self.target.dtype)

        def arrive(self):
            pl.when(self.origin)(self.copy.wait_recv)

        def drain(self):
            pl.when(self.to)(self.copy.wait_send)

    traces_x = Exchange(0, -1, 0, lifted.at[0, 0], halo_x)
    flags_x = Exchange(1, -1, 0, keep.at[0, 0], keep_x)
    traces_y = Exchange(2, 0, -1, lifted.at[1, :, 0], halo_y)
    flags_y = Exchange(3, 0, -1, keep.at[1, :, 0], keep_y)
    first = [traces_x, flags_x, traces_y, flags_y]
    for exchange in first:
        exchange.start()

    terms_x = Exchange(4, 1, 0, send_x, recv_x)
    terms_y = Exchange(5, 0, 1, send_y, recv_y)
    rims = {}
    for slot, (dx, dy) in enumerate(around):
        edge_x = {-1: 0, 1: wx}.get(dx)
        edge_y = {-1: 0, 1: wy}.get(dy)
        if dy == 0:
            source, target = vertex.at[edge_x], rim_x.at[(dx + 1) // 2]
        elif dx == 0:
            source, target = vertex.at[:, edge_y], rim_y.at[(dy + 1) // 2]
        else:
            source, target = vertex.at[edge_x, edge_y], rim_c.at[(dx + 1) // 2, (dy + 1) // 2]
        rims[dx, dy] = Exchange(6 + slot, dx, dy, source, target)

    lane = lax.broadcasted_iota(jnp.int32, (8, depth), 1)
    row = lax.broadcasted_iota(jnp.int32, (8, depth), 0)
    lane_faces = lax.broadcasted_iota(jnp.int32, (faces, depth), 1)

    def next_flag(x, y, d):
        if d == 0:
            return keep[0, x + 1, y] if x + 1 < wx else keep_x[y]
        if d == 1:
            return keep[1, x, y + 1] if y + 1 < wy else keep_y[x]
        flag = jnp.broadcast_to(keep[2, x, y], (8, depth))
        return jnp.where(lane == depth - 1, 0.0, pltpu.roll(flag, depth - 1, 1))[:1]

    corners = {}

    def process(columns):
        pieces = []
        for x, y in columns:
            low_z = lifted[2, x, y].astype(jnp.float32)
            high_z = jnp.where(lane_faces == depth - 1, 0.0, pltpu.roll(low_z, depth - 1, 1)).astype(jnp.bfloat16)
            pieces.append(
                jnp.concatenate(
                    [
                        lifted[0, x, y],
                        lifted[0, x + 1, y] if x + 1 < wx else halo_x[y],
                        lifted[1, x, y],
                        lifted[1, x, y + 1] if y + 1 < wy else halo_y[x],
                        lifted[2, x, y],
                        high_z,
                    ],
                    axis=0,
                )
            )
        element = jnp.concatenate(pieces, axis=1)
        interior = lax.dot_general(
            solve_t[...], element, (((0,), (0,)), ((), ())), preferred_element_type=jnp.float32
        ).astype(jnp.bfloat16)
        flux = jnp.dot(flux_map[...], interior, preferred_element_type=jnp.float32)
        rounded = []
        for index, (x, y) in enumerate(columns):
            lanes = slice(index * depth, (index + 1) * depth)
            parts = []
            for face_slot in range(6):
                rows = slice(face_slot * faces, (face_slot + 1) * faces)
                d, outward = face_slot // 2, face_slot % 2
                flag = next_flag(x, y, d) if outward else keep[d, x, y]
                scale = visc[x, y] * flag
                parts.append((flux[rows, lanes] + penalty * pieces[index][rows].astype(jnp.float32)) * scale)
            residual[0, x, y] = parts[0]
            residual[1, x, y] = parts[2]
            residual[2, x, y] = parts[4] + pltpu.roll(parts[5], 1, 1)
            cut = jnp.concatenate(parts, axis=0).astype(jnp.bfloat16)
            if x + 1 < wx:
                high[0, x, y] = parts[1]
            else:
                send_x[y] = cut[faces : 2 * faces]
            if y + 1 < wy:
                high[1, x, y] = parts[3]
            else:
                send_y[x] = cut[3 * faces : 4 * faces]
            rounded.append(cut)
        both = jnp.dot(gather[...], jnp.concatenate(rounded, axis=1), preferred_element_type=jnp.float32)
        sums = both[:32] + both[32:]
        for index, (x, y) in enumerate(columns):
            for dx, dy in itertools.product(range(2), range(2)):
                part = sums[16 * dx + 8 * dy : 16 * dx + 8 * dy + 8, index * depth : (index + 1) * depth]
                key = (x + dx, y + dy)
                corners[key] = part if key not in corners else corners[key] + part

    everything = list(itertools.product(range(wx), range(wy)))
    inner = [(x, y) for x, y in everything if x + 1 < wx and y + 1 < wy]
    need_x = [(x, y) for x, y in everything if x + 1 == wx and y + 1 < wy]
    need_y = [(x, y) for x, y in everything if y + 1 == wy]
    early = len(inner) // 4 * 4
    for start in range(0, early, 4):
        process(inner[start : start + 4])
    traces_x.arrive()
    flags_x.arrive()
    process(inner[early:] + need_x)
    traces_y.arrive()
    flags_y.arrive()
    process(need_y)

    for x, y in itertools.product(range(wx + 1), range(wy + 1)):
        value = corners[x, y]
        above = pltpu.roll(jnp.where(lane == depth - 1, 0.0, value), 1, 1)
        value = value + pltpu.roll(above, 4, 0)
        if x < wx and y < wy:
            vertex[x, y] = jnp.where(row == CORNER - 1, diag[x, y], value)
        else:
            vertex[x, y] = jnp.where(row == CORNER - 1, 0.0, value)
    for exchange in rims.values():
        exchange.start()
    terms_x.start()
    terms_y.start()

    for x, y in everything:
        if x:
            residual[0, x, y] += high[0, x - 1, y]
        if y:
            residual[1, x, y] += high[1, x, y - 1]

    for exchange in rims.values():
        exchange.arrive()
    fixes = {}
    for x, y in itertools.product(range(wx + 1), range(wy + 1)):
        value = vertex[x, y]
        side_x = {0: 1, wx: 0}.get(x)
        side_y = {0: 1, wy: 0}.get(y)
        if side_x is not None:
            value = value + rim_x[side_x, y]
        if side_y is not None:
            value = value + rim_y[side_y, x]
        if side_x is not None and side_y is not None:
            value = value + rim_c[side_x, side_y]
        inside = present(int(x == wx), int(y == wy))
        below = jnp.broadcast_to(value[CORNER - 1 : CORNER], value.shape)
        if inside is not None:
            value = jnp.where(inside, value, 0.0)
            below = jnp.where(inside, below, 1.0)
        fix = value / below
        above = jnp.where(lane == depth - 1, 0.0, pltpu.roll(fix, depth - 1, 1))
        fixes[x, y] = jnp.where(row < CORNER, fix, pltpu.roll(above, 4, 0))

    terms_x.arrive()
    terms_y.arrive()
    for x in range(wx):
        stacks = []
        for y in range(wy):
            value = jnp.concatenate([fixes[x, y], fixes[x, y + 1], fixes[x + 1, y], fixes[x + 1, y + 1]], axis=0)
            upper = value.astype(jnp.bfloat16)
            lower = (value - upper.astype(jnp.float32)).astype(jnp.bfloat16)
            stacks.append(jnp.concatenate([upper, lower, upper], axis=0))
        lift = jnp.dot(spread[...], jnp.concatenate(stacks, axis=1), preferred_element_type=jnp.float32)
        for y in range(wy):
            for d in range(3):
                value = residual[d, x, y]
                if d == 0 and x == 0:
                    value = value + recv_x[y].astype(jnp.float32)
                if d == 1 and y == 0:
                    value = value + recv_y[x].astype(jnp.float32)
                piece = lift[d * faces : (d + 1) * faces, y * depth : (y + 1) * depth]
                out[d, x, y] = (value + keep[d, x, y] * piece).astype(jnp.bfloat16)

    for exchange in first + list(rims.values()) + [terms_x, terms_y]:
        exchange.drain()


def cell_viscosity(visc_class, viscosity):
    result = jnp.zeros(visc_class.shape, jnp.float32)
    for level in range(viscosity.shape[0]):
        result = result + jnp.where(visc_class == level, viscosity[level], jnp.float32(0.0))
    return result


def local(count_x, count_y, traces, dirichlet, visc_class, viscosity, coarse_diag, solve_map, flux_map):
    faces, wx, wy, depth = traces.shape[1:]
    keep = (1 - dirichlet).astype(jnp.bfloat16)
    lifted = jnp.transpose(traces, (0, 2, 3, 1, 4)) * keep[:, :, :, None]
    operands = (
        lifted,
        keep.astype(jnp.float32)[:, :, :, None],
        cell_viscosity(visc_class, viscosity)[:, :, None],
        coarse_diag[:, :, None],
        solve_map.T,
        flux_map,
        jnp.asarray(gather_table()),
        jnp.asarray(spread_table()),
    )
    whole = pl.BlockSpec(memory_space=pltpu.VMEM)
    exchanges = 14
    result = pl.pallas_call(
        functools.partial(kernel, count_x, count_y),
        out_shape=jax.ShapeDtypeStruct((3, wx, wy, faces, depth), jnp.bfloat16),
        in_specs=[whole] * len(operands),
        out_specs=whole,
        scratch_shapes=[
            pltpu.VMEM((wy, faces, depth), jnp.bfloat16),
            pltpu.VMEM((wx, faces, depth), jnp.bfloat16),
            pltpu.VMEM((wy, 1, depth), jnp.float32),
            pltpu.VMEM((wx, 1, depth), jnp.float32),
            pltpu.VMEM((3, wx, wy, faces, depth), jnp.float32),
            pltpu.VMEM((2, wx, wy, faces, depth), jnp.float32),
            pltpu.VMEM((wy, faces, depth), jnp.bfloat16),
            pltpu.VMEM((wx, faces, depth), jnp.bfloat16),
            pltpu.VMEM((wy, faces, depth), jnp.bfloat16),
            pltpu.VMEM((wx, faces, depth), jnp.bfloat16),
            pltpu.VMEM((wx + 1, wy + 1, 8, depth), jnp.float32),
            pltpu.VMEM((2, wy + 1, 8, depth), jnp.float32),
            pltpu.VMEM((2, wx + 1, 8, depth), jnp.float32),
            pltpu.VMEM((2, 2, 8, depth), jnp.float32),
            pltpu.SemaphoreType.DMA((exchanges,)),
            pltpu.SemaphoreType.DMA((exchanges,)),
        ],
        compiler_params=pltpu.CompilerParams(collective_id=0, has_side_effects=True),
        name="apply",
    )(*operands)
    return jnp.transpose(result, (0, 3, 1, 2, 4))


def solution(mesh):
    count_x, count_y = mesh.shape["gx"], mesh.shape["gy"]
    in_specs = (
        P(None, None, "gx", "gy", None),
        P(None, "gx", "gy", None),
        P("gx", "gy", None),
        P(),
        P("gx", "gy", None),
        P(),
        P(),
    )
    out_specs = P(None, None, "gx", "gy", None)
    return jax.shard_map(
        functools.partial(local, count_x, count_y), mesh=mesh, in_specs=in_specs, out_specs=out_specs, check_vma=False
    )
```

time: 73.7 us -> 29 us (0.39)
  the two profiles are of different devices: /device:TPU:191 before, /device:TPU:320 now
where the time goes in v1:
time: 29 us; the launch traced here: 28.7 us
  Pallas kernels  19.6 us (68%)
  other arithmetic  5.63 us (19%)
  local copies, waits for them, and re-layouts  3.53 us (12%)
    pallas_call x1, Pallas kernels, local(): pl.pallas_call(functools.partial(kernel, count_x, count_y), out_shape=jax...  19.6 us
    add x1, other arithmetic, cell_viscosity(): result + jnp.where(visc_class == level, viscosity[level], jnp.float32(0.0))  3.03 us
    transpose x1, local copies, waits for them, and re-layouts, local(): return jnp.transpose(result, (0, 3, 1, 2, 4))  2.11 us
    mul x1, other arithmetic, local(): lifted = jnp.transpose(traces, (0, 2, 3, 1, 4)) * keep[:, :, :, None]  1.99 us
    slice x1, local copies, waits for them, and re-layouts, cell_viscosity(): viscosity[level]  1.42 us
    broadcast_in_dim x1, other arithmetic, local(): keep.astype(jnp.float32)[:, :, :, None]  0.61 us

profile of v1, /device:TPU:320, one launch (start us, length us, event | category | flops | bytes accessed | tf_op | source)
XLA Modules:
  0.0 28.7 jit_solution(9630263690885743809)
XLA Ops:
  0.0 0.0 copy-start.1
  0.0 0.0 copy-start
  0.0 1.4 %fusion.2 = (f32[1]{0:T(128)}, f32[1]{0:T(128)}, f32[1]{0:T(128)}, f32[1]{0:T(128)}) fusion(f32[4]{0:T(128)} %param.12), kind=kLoop, calls=%fused_computation.5 | loop fusion | bytes 32 | tf_op jit(solution)/shard_map/slice | solution.py:286
  1.4 0.0 copy-done.1
  1.4 3.0 %select_add_fusion = f32[4,4,128]{2,1,0:T(4,128)} fusion(s32[4,4,128]{2,1,0:T(4,128)S(1)} %copy-done.1, f32[]{:T(128)} %bitcast.5, f32[]{:T(128)} %bitcast.4, f32[]{:T(128)} %bitcast.3, f32[]{:T(128)} %bitcast.2), kind=kLoop, calls=%fused_computation.3 | loop fusion | flops 22528 | bytes 16400 | tf_op jit(solution)/shard_map/add | solution.py:286
  4.5 0.0 copy-done
  4.5 0.6 %fusion.1 = (f32[3,4,4,128]{3,2,1,0:T(4,128)}, bf16[3,4,4,128]{3,2,1,0:T(4,128)(2,1)S(1)}) fusion(s32[3,4,4,128]{3,2,1,0:T(4,128)S(1)} %copy-done), kind=kLoop, calls=%fused_computation.4 | loop fusion | flops 18432 | bytes 61440 | tf_op jit(solution)/shard_map/broadcast_in_dim | solution.py:296
  5.1 2.0 %fusion.lifted = bf16[3,4,4,48,128]{4,3,2,1,0:T(8,128)(2,1)} fusion(bf16[3,48,4,4,128]{4,3,2,1,0:T(4,128)(2,1)} %param.9, bf16[3,4,4,128]{3,2,1,0:T(4,128)(2,1)S(1)} %get-tuple-element.6), kind=kLoop, calls=%fused_computation.1 | loop fusion | flops 294912 | bytes 1191936 | tf_op jit(solution)/shard_map/mul | solution.py:293
  7.1 19.6 %apply.1 = bf16[3,4,4,48,128]{4,3,2,1,0:T(8,128)(2,1)} custom-call(bf16[3,4,4,48,128]{4,3,2,1,0:T(8,128)(2,1)} %fusion.lifted, f32[3,4,4,1,128]{4,3,2,1,0:T(1,128)} %bitcast.13, f32[4,4,1,128]{3,2,1,0:T(1,128)} %bitcast.14, f32[4,4,1,128]{3,2,1,0:T(1,128)} %bitcast.15, bf16[288,256]{1,0:T(8,128)(2,1)} %bitcast.12, bf16[288,256]{1,0:T(8,128)(2,1)} %flux_map.1, ...), custom_call_target="tpu_custom_call" | custom-call | tf_op jit(solution)/shard_map/apply/pallas_call | solution.py:306
  26.6 2.1 %copy.11 = bf16[3,48,4,4,128]{4,3,2,1,0:T(4,128)(2,1)} copy(bf16[3,48,4,4,128]{4,1,3,2,0:T(8,128)(2,1)} %bitcast.11) | data formatting | bytes 1179648 | tf_op jit(solution)/shard_map/transpose | solution.py:332
Async XLA Ops:
  0.0 1.4 %copy-start.1 = (s32[4,4,128]{2,1,0:T(4,128)S(1)}, s32[4,4,128]{2,1,0:T(4,128)}, u32[]{:S(2)}) copy-start(s32[4,4,128]{2,1,0:T(4,128)} %param.11) | copy-start | bytes 24580
  0.0 4.5 %copy-start = (s32[3,4,4,128]{3,2,1,0:T(4,128)S(1)}, s32[3,4,4,128]{3,2,1,0:T(4,128)}, u32[]{:S(2)}) copy-start(s32[3,4,4,128]{3,2,1,0:T(4,128)} %param.10) | copy-start | bytes 73732

commit v2 on v1

v2 whole, which is shorter than its diff:
```python
import functools
import itertools
import math

import jax
import jax.numpy as jnp
import ml_dtypes
import numpy as np
from jax import lax
from jax.experimental import pallas as pl
from jax.experimental.pallas import tpu as pltpu
from jax.sharding import PartitionSpec as P

MESH = pl.DeviceIdType.MESH
penalty = 0.5
CORNER = 4


def corner_table():
    points = [-1.0, -math.sqrt(0.2), math.sqrt(0.2), 1.0]
    table = np.zeros((16, 4), np.float64)
    for a, b, p, q in itertools.product(range(4), range(4), range(2), range(2)):
        table[4 * a + b, 2 * p + q] = (1 + (2 * p - 1) * points[a]) * (1 + (2 * q - 1) * points[b]) / 4
    return table.astype(np.float32)


def in_two(table):
    high = table.astype(ml_dtypes.bfloat16)
    low = (table - high.astype(np.float32)).astype(ml_dtypes.bfloat16)
    return high, low


def gather_table():
    weights = corner_table()
    table = np.zeros((32, 6, 3, 16), np.float32)
    for dx, dy, dz, m in itertools.product(range(2), range(2), range(2), range(3)):
        row = 16 * dx + 8 * dy + CORNER * dz + m
        table[row, dx, m] = weights[:, 2 * dy + dz]
        table[row, 2 + dy, m] = weights[:, 2 * dx + dz]
        table[row, 4 + dz, m] = weights[:, 2 * dx + dy]
    return np.concatenate(in_two(table.reshape(32, 288)), axis=0)


def spread_table():
    weights = corner_table()
    table = np.zeros((3, 3, 16, 32), np.float32)
    for dx, dy, dz, m in itertools.product(range(2), range(2), range(2), range(3)):
        column = 16 * dx + 8 * dy + CORNER * dz + m
        if dx == 0:
            table[0, m, :, column] = weights[:, 2 * dy + dz]
        if dy == 0:
            table[1, m, :, column] = weights[:, 2 * dx + dz]
        if dz == 0:
            table[2, m, :, column] = weights[:, 2 * dx + dy]
    high, low = in_two(table.reshape(144, 32))
    return np.concatenate([high, high, low], axis=1)


def one_hot(rows):
    i = lax.broadcasted_iota(jnp.int32, (rows, rows), 0)
    j = lax.broadcasted_iota(jnp.int32, (rows, rows), 1)
    hit = jnp.logical_and((i & 15) == (j >> 4), (i >> 4) == (j & 15))
    return jnp.where(hit, 1.0, 0.0).astype(jnp.bfloat16)


def kernel(
    count_x, count_y, wx, wy,
    traces_hbm, dirichlet_hbm, class_hbm, viscosity_hbm, diag_hbm, solve_hbm, flux_hbm, gather_hbm, spread_hbm,
    out_hbm,
    traces, dirichlet, classes, viscosity, diag, solve_t, flux_map, gather, spread, result,
    swap, solve_map, lifted, keep, scale, halo_x, halo_y, first_y, flag_x, flag_y, keep_x, keep_y,
    residual, high, final, send_x, send_y, recv_x, recv_y,
    edge_x, edge_y, edge_c, rim_x, rim_y, rim_c,
    load_sem, store_sem, send_sem, recv_sem, ready,
):
    columns, depth = wx * wy, traces.shape[3]
    faces = traces.shape[1]
    groups = faces // 16
    me_x, me_y = lax.axis_index("gx"), lax.axis_index("gy")
    there = {-1: (me_x > 0, me_y > 0), 0: (None, None), 1: (me_x < count_x - 1, me_y < count_y - 1)}

    def present(dx, dy):
        a, b = there[dx][0], there[dy][1]
        if a is None:
            return b
        return a if b is None else jnp.logical_and(a, b)

    def device(dx, dy):
        return {"gx": me_x + dx, "gy": me_y + dy}

    around = [(-1, -1), (1, -1), (-1, 1), (1, 1), (0, -1), (0, 1), (-1, 0), (1, 0)]
    barrier = pltpu.get_barrier_semaphore()
    total = 0
    for dx, dy in around[4:]:
        here = present(dx, dy)
        total = total + here.astype(jnp.int32)

        @pl.when(here)
        def _():
            pl.semaphore_signal(barrier, inc=1, device_id=device(dx, dy), device_id_type=MESH)

    loads = [
        (dirichlet_hbm, dirichlet), (traces_hbm.at[0], traces.at[0]), (traces_hbm.at[1], traces.at[1]),
        (traces_hbm.at[2], traces.at[2]), (viscosity_hbm, viscosity), (class_hbm, classes), (solve_hbm, solve_t),
        (flux_hbm, flux_map), (gather_hbm, gather), (diag_hbm, diag), (spread_hbm, spread),
    ]
    loads = [pltpu.make_async_copy(a, b, load_sem.at[i]) for i, (a, b) in enumerate(loads)]
    for load in loads:
        load.start()

    class Exchange:
        def __init__(self, slot, dx, dy, source, target):
            self.to, self.origin, self.target = present(dx, dy), present(-dx, -dy), target
            self.copy = pltpu.make_async_remote_copy(
                src_ref=source, dst_ref=target, send_sem=send_sem.at[slot], recv_sem=recv_sem.at[slot],
                device_id=device(dx, dy), device_id_type=MESH,
            )

        def clear(self):
            @pl.when(jnp.logical_not(self.origin))
            def _():
                self.target[...] = jnp.zeros(self.target.shape, self.target.dtype)

        def start(self):
            pl.when(self.to)(self.copy.start)

        def arrive(self):
            pl.when(self.origin)(self.copy.wait_recv)

        def drain(self):
            pl.when(self.to)(self.copy.wait_send)

    traces_x = Exchange(0, -1, 0, lifted.at[0, pl.ds(0, wy)], halo_x)
    flags_x = Exchange(1, -1, 0, flag_x, keep_x)
    traces_y = Exchange(2, 0, -1, first_y, halo_y)
    flags_y = Exchange(3, 0, -1, flag_y, keep_y)
    terms_x = Exchange(4, 1, 0, send_x, recv_x)
    terms_y = Exchange(5, 0, 1, send_y, recv_y)
    first = [flags_y, traces_y, flags_x, traces_x]
    rims = []
    for slot, (dx, dy) in enumerate(around):
        if dy == 0:
            source, target = edge_x.at[(dx + 1) // 2], rim_x.at[(dx + 1) // 2]
        elif dx == 0:
            source, target = edge_y.at[(dy + 1) // 2], rim_y.at[(dy + 1) // 2]
        else:
            source, target = edge_c.at[(dx + 1) // 2, (dy + 1) // 2], rim_c.at[(dx + 1) // 2, (dy + 1) // 2]
        rims.append(Exchange(6 + slot, dx, dy, source, target))
    for exchange in first + [terms_x, terms_y] + rims:
        exchange.clear()

    swap[...] = one_hot(256)
    lane = lax.broadcasted_iota(jnp.int32, (8, depth), 1)
    row = lax.broadcasted_iota(jnp.int32, (8, depth), 0)
    lane_faces = lax.broadcasted_iota(jnp.int32, (faces, depth), 1)

    def to_columns(pairs):
        moved = jnp.concatenate([traces[d, 16 * g : 16 * g + 16].reshape(256, depth) for d, g in pairs], axis=1)
        moved = jnp.dot(swap[...], moved, preferred_element_type=jnp.float32)
        for index, (d, g) in enumerate(pairs):
            for c in range(columns):
                piece = moved[16 * c : 16 * c + 16, index * depth : (index + 1) * depth]
                lifted[d, c, 16 * g : 16 * g + 16] = (piece * keep[d, c : c + 1]).astype(jnp.bfloat16)

    def in_pairs(items):
        return [items[i : i + 2] for i in range(0, len(items), 2)]

    loads[0].wait()
    keep[...] = 1.0 - dirichlet[...].astype(jnp.float32)
    flag_x[...] = keep[0, :wy]
    for x in range(wx):
        flag_y[x : x + 1] = keep[1, x * wy : x * wy + 1]
    loads[1].wait()
    loads[2].wait()
    for pair in in_pairs([(d, g) for d in (1, 0) for g in range(groups)]):
        to_columns(pair)
    for x in range(wx):
        first_y[x] = lifted[1, x * wy]
    pl.semaphore_wait(barrier, total)
    for exchange in first:
        exchange.start()
    for dx in (-1, 1):

        @pl.when(present(dx, 0))
        def _():
            pl.semaphore_signal(ready, inc=1, device_id=device(dx, 0), device_id_type=MESH)

    loads[3].wait()
    for pair in in_pairs([(2, g) for g in range(groups)]):
        to_columns(pair)
    for load in loads[4:7]:
        load.wait()
    solve_map[...] = solve_t[...].T
    visc = jnp.zeros(classes.shape, jnp.float32)
    for level in range(viscosity.shape[0]):
        visc = visc + jnp.where(classes[...] == level, viscosity[level], 0.0)
    lanes_c = lax.broadcasted_iota(jnp.int32, (columns, depth), 1)
    for d in range(3):
        scale[2 * d] = visc * keep[d]
    scale[5] = visc * jnp.where(lanes_c == depth - 1, 0.0, pltpu.roll(keep[2], depth - 1, 1))
    scale[1, : columns - wy] = visc[: columns - wy] * keep[0, wy:]
    scale[3, : columns - 1] = visc[: columns - 1] * keep[1, 1:]
    for load in loads[7:]:
        load.wait()

    corners = {}

    def process(chosen, after_terms=lambda: None):
        pieces = []
        for c in chosen:
            x, y = c // wy, c % wy
            low_z = lifted[2, c].astype(jnp.float32)
            high_z = jnp.where(lane_faces == depth - 1, 0.0, pltpu.roll(low_z, depth - 1, 1)).astype(jnp.bfloat16)
            pieces.append(
                jnp.concatenate(
                    [
                        lifted[0, c],
                        lifted[0, c + wy] if x + 1 < wx else halo_x[y],
                        lifted[1, c],
                        lifted[1, c + 1] if y + 1 < wy else halo_y[x],
                        lifted[2, c],
                        high_z,
                    ],
                    axis=0,
                )
            )
        element = jnp.concatenate(pieces, axis=1)
        interior = jnp.dot(solve_map[...], element, preferred_element_type=jnp.float32).astype(jnp.bfloat16)
        flux = jnp.dot(flux_map[...], interior, preferred_element_type=jnp.float32)
        rounded = []
        for index, c in enumerate(chosen):
            x, y = c // wy, c % wy
            lanes = slice(index * depth, (index + 1) * depth)
            parts = []
            for face_slot in range(6):
                rows = slice(face_slot * faces, (face_slot + 1) * faces)
                term = flux[rows, lanes] + penalty * pieces[index][rows].astype(jnp.float32)
                parts.append(term * scale[face_slot, c : c + 1])
            residual[0, c] = parts[0]
            residual[1, c] = parts[2]
            residual[2, c] = parts[4] + pltpu.roll(parts[5], 1, 1)
            cut = jnp.concatenate(parts, axis=0).astype(jnp.bfloat16)
            if x + 1 < wx:
                high[0, c] = parts[1]
            else:
                send_x[y] = cut[faces : 2 * faces]
            if y + 1 < wy:
                high[1, c] = parts[3]
            else:
                send_y[x] = cut[3 * faces : 4 * faces]
            rounded.append(cut)
        after_terms()
        both = jnp.dot(gather[...], jnp.concatenate(rounded, axis=1), preferred_element_type=jnp.float32)
        sums = both[:32] + both[32:]
        for index, c in enumerate(chosen):
            x, y = c // wy, c % wy
            for dx, dy in itertools.product(range(2), range(2)):
                part = sums[16 * dx + 8 * dy : 16 * dx + 8 * dy + 8, index * depth : (index + 1) * depth]
                key = (x + dx, y + dy)
                corners[key] = part if key not in corners else corners[key] + part

    inner = [c for c in range(columns) if c + wy < columns and c % wy + 1 < wy]
    need_x = [c for c in range(columns) if c + wy >= columns and c % wy + 1 < wy]
    need_y = [c for c in range(columns) if c % wy + 1 == wy]
    early = len(inner) // 4 * 4
    for start in range(0, early, 4):
        process(inner[start : start + 4])
    flags_x.arrive()
    traces_x.arrive()
    scale[1, columns - wy :] = visc[columns - wy :] * keep_x[...]
    process(inner[early:] + need_x)
    flags_y.arrive()
    traces_y.arrive()
    for x in range(wx):
        c = x * wy + wy - 1
        scale[3, c : c + 1] = visc[c : c + 1] * keep_y[x : x + 1]

    def terms_out():
        terms_y.start()
        terms_x.start()

    process(need_y, terms_out)

    vertices = list(itertools.product(range(wx + 1), range(wy + 1)))
    for x, y in vertices:
        value = corners[x, y]
        above = pltpu.roll(jnp.where(lane == depth - 1, 0.0, value), 1, 1)
        value = value + pltpu.roll(above, 4, 0)
        if x < wx and y < wy:
            corners[x, y] = jnp.where(row == CORNER - 1, diag[x * wy + y : x * wy + y + 1], value)
        else:
            corners[x, y] = jnp.where(row == CORNER - 1, 0.0, value)

    def pack(target, values):
        for i in range(0, len(values), 2):
            value = values[i]
            if i + 1 < len(values):
                value = jnp.where(row < CORNER, value, pltpu.roll(values[i + 1], 4, 0))
            target[i // 2] = value

    for side in range(2):
        for other in range(2):
            edge_c[side, other] = corners[side * wx, other * wy]
    for side in range(2):
        pack(edge_y.at[side], [corners[x, side * wy] for x in range(wx + 1)])
        pack(edge_x.at[side], [corners[side * wx, y] for y in range(wy + 1)])
    pl.semaphore_wait(ready, there[-1][0].astype(jnp.int32) + there[1][0].astype(jnp.int32))
    for exchange in rims:
        exchange.start()

    for c in range(columns):
        if c >= wy:
            residual[0, c] += high[0, c - wy]
        if c % wy:
            residual[1, c] += high[1, c - 1]

    for exchange in rims:
        exchange.arrive()

    def unpack(source, index):
        value = source[index // 2]
        return pltpu.roll(value, 4, 0) if index % 2 else value

    fixes = {}
    for x, y in vertices:
        value = corners[x, y]
        side_x = {0: 0, wx: 1}.get(x)
        side_y = {0: 0, wy: 1}.get(y)
        if side_x is not None:
            value = value + unpack(rim_x.at[1 - side_x], y)
        if side_y is not None:
            value = value + unpack(rim_y.at[1 - side_y], x)
        if side_x is not None and side_y is not None:
            value = value + rim_c[1 - side_x, 1 - side_y]
        inside = present(int(x == wx), int(y == wy))
        below = jnp.broadcast_to(value[CORNER - 1 : CORNER], value.shape)
        if inside is not None:
            value = jnp.where(inside, value, 0.0)
            below = jnp.where(inside, below, 1.0)
        fix = value / below
        above = jnp.where(lane == depth - 1, 0.0, pltpu.roll(fix, depth - 1, 1))
        fixes[x, y] = jnp.where(row < CORNER, fix, pltpu.roll(above, 4, 0))

    stacks = []
    for c in range(columns):
        x, y = c // wy, c % wy
        value = jnp.concatenate([fixes[x, y], fixes[x, y + 1], fixes[x + 1, y], fixes[x + 1, y + 1]], axis=0)
        upper = value.astype(jnp.bfloat16)
        lower = (value - upper.astype(jnp.float32)).astype(jnp.bfloat16)
        stacks.append(jnp.concatenate([upper, lower, upper], axis=0))
    stores = []
    for d in (2, 0, 1):
        if d == 0:
            terms_x.arrive()
        if d == 1:
            terms_y.arrive()
        for start in range(0, columns, 4):
            chosen = range(start, start + 4)
            lift = jnp.dot(
                spread[d * faces : (d + 1) * faces],
                jnp.concatenate([stacks[c] for c in chosen], axis=1),
                preferred_element_type=jnp.float32,
            )
            for index, c in enumerate(chosen):
                x, y = c // wy, c % wy
                value = residual[d, c]
                if d == 0 and x == 0:
                    value = value + recv_x[y].astype(jnp.float32)
                if d == 1 and y == 0:
                    value = value + recv_y[x].astype(jnp.float32)
                piece = lift[:, index * depth : (index + 1) * depth]
                final[d, c] = (value + keep[d, c : c + 1] * piece).astype(jnp.bfloat16)
        for pair in in_pairs(list(range(groups))):
            moved = jnp.concatenate(
                [final[d, :, 16 * g : 16 * g + 16].reshape(256, depth) for g in pair], axis=1
            )
            moved = jnp.dot(swap[...], moved, preferred_element_type=jnp.float32).astype(jnp.bfloat16)
            for index, g in enumerate(pair):
                piece = moved[:, index * depth : (index + 1) * depth]
                result[d, 16 * g : 16 * g + 16] = piece.reshape(16, columns, depth)
        stores.append(pltpu.make_async_copy(result.at[d], out_hbm.at[d], store_sem.at[d]))
        stores[-1].start()

    for exchange in first + rims + [terms_x, terms_y]:
        exchange.drain()
    for store in stores:
        store.wait()


def local(count_x, count_y, traces, dirichlet, visc_class, viscosity, coarse_diag, solve_map, flux_map):
    faces, wx, wy, depth = traces.shape[1:]
    columns = wx * wy
    inner = solve_map.shape[0]
    operands = (
        traces.reshape(3, faces, columns, depth),
        dirichlet.reshape(3, columns, depth),
        visc_class.reshape(columns, depth),
        viscosity,
        coarse_diag.reshape(columns, depth),
        solve_map.T,
        flux_map,
        jnp.asarray(gather_table()),
        jnp.asarray(spread_table()),
    )
    anywhere = pl.BlockSpec(memory_space=pl.ANY)
    exchanges = 14
    rims_x, rims_y = wy // 2 + 1, wx // 2 + 1
    f32, bf16 = jnp.float32, jnp.bfloat16
    scratch = [
        pltpu.SMEM(a.shape, a.dtype) if index == 3 else pltpu.VMEM(a.shape, a.dtype) for index, a in enumerate(operands)
    ] + [
        pltpu.VMEM((3, faces, columns, depth), bf16),
        pltpu.VMEM((256, 256), bf16),
        pltpu.VMEM((inner, 6 * faces), bf16),
        pltpu.VMEM((3, columns, faces, depth), bf16),
        pltpu.VMEM((3, columns, depth), f32),
        pltpu.VMEM((6, columns, depth), f32),
        pltpu.VMEM((wy, faces, depth), bf16),
        pltpu.VMEM((wx, faces, depth), bf16),
        pltpu.VMEM((wx, faces, depth), bf16),
        pltpu.VMEM((wy, depth), f32),
        pltpu.VMEM((wx, depth), f32),
        pltpu.VMEM((wy, depth), f32),
        pltpu.VMEM((wx, depth), f32),
        pltpu.VMEM((3, columns, faces, depth), f32),
        pltpu.VMEM((2, columns, faces, depth), f32),
        pltpu.VMEM((3, columns, faces, depth), bf16),
        pltpu.VMEM((wy, faces, depth), bf16),
        pltpu.VMEM((wx, faces, depth), bf16),
        pltpu.VMEM((wy, faces, depth), bf16),
        pltpu.VMEM((wx, faces, depth), bf16),
        pltpu.VMEM((2, rims_x, 8, depth), f32),
        pltpu.VMEM((2, rims_y, 8, depth), f32),
        pltpu.VMEM((2, 2, 8, depth), f32),
        pltpu.VMEM((2, rims_x, 8, depth), f32),
        pltpu.VMEM((2, rims_y, 8, depth), f32),
        pltpu.VMEM((2, 2, 8, depth), f32),
        pltpu.SemaphoreType.DMA((len(operands) + 2,)),
        pltpu.SemaphoreType.DMA((3,)),
        pltpu.SemaphoreType.DMA((exchanges,)),
        pltpu.SemaphoreType.DMA((exchanges,)),
        pltpu.SemaphoreType.REGULAR,
    ]
    result = pl.pallas_call(
        functools.partial(kernel, count_x, count_y, wx, wy),
        out_shape=jax.ShapeDtypeStruct((3, faces, columns, depth), bf16),
        in_specs=[anywhere] * len(operands),
        out_specs=anywhere,
        scratch_shapes=scratch,
        compiler_params=pltpu.CompilerParams(collective_id=0, has_side_effects=True),
        name="apply",
    )(*operands)
    return result.reshape(3, faces, wx, wy, depth)


def solution(mesh):
    count_x, count_y = mesh.shape["gx"], mesh.shape["gy"]
    in_specs = (
        P(None, None, "gx", "gy", None),
        P(None, "gx", "gy", None),
        P("gx", "gy", None),
        P(),
        P("gx", "gy", None),
        P(),
        P(),
    )
    out_specs = P(None, None, "gx", "gy", None)
    return jax.shard_map(
        functools.partial(local, count_x, count_y), mesh=mesh, in_specs=in_specs, out_specs=out_specs, check_vma=False
    )
```

time: 29 us -> 20.9 us (0.72)
  other arithmetic: 5.63 us -> 0 us
  local copies, waits for them, and re-layouts: 3.53 us -> 2.08 us
  Pallas kernels: 19.6 us -> 18.6 us
    add x1 -> x0, other arithmetic: 3.03 us -> none  [cell_viscosity(): result + jnp.where(visc_class == level, viscosity[level], jnp.float32(0.0))]
    transpose x1 -> x0, local copies, waits for them, and re-layouts: 2.11 us -> none  [local(): return jnp.transpose(result, (0, 3, 1, 2, 4))]
    unnamed x4 -> x1, local copies, waits for them, and re-layouts: 0.01 us -> 2.08 us
    mul x1 -> x0, other arithmetic: 1.99 us -> none  [local(): lifted = jnp.transpose(traces, (0, 2, 3, 1, 4)) * keep[:, :, :, None]]
    slice x1 -> x0, local copies, waits for them, and re-layouts: 1.42 us -> none  [cell_viscosity(): viscosity[level]]
    pallas_call x1, Pallas kernels: 19.6 us -> 18.6 us  [local(): pl.pallas_call(functools.partial(kernel, count_x, count_y, wx, wy), out_s...]
    broadcast_in_dim x1 -> x0, other arithmetic: 0.61 us -> none  [local(): keep.astype(jnp.float32)[:, :, :, None]]
where the time goes in v2:
time: 20.9 us; the launch traced here: 20.7 us
  Pallas kernels  18.6 us (89%)
  local copies, waits for them, and re-layouts  2.08 us (10%)
    pallas_call x1, Pallas kernels, local(): pl.pallas_call(functools.partial(kernel, count_x, count_y, wx, wy), out_s...  18.6 us
    unnamed x1, local copies, waits for them, and re-layouts  2.08 us

profile of v2, /device:TPU:320, one launch (start us, length us, event | category | flops | bytes accessed | tf_op | source)
XLA Modules:
  0.0 20.7 jit_solution(6249691521706448046)
XLA Ops:
  0.0 18.6 %apply.1 = bf16[3,48,16,128]{3,2,1,0:T(8,128)(2,1)} custom-call(bf16[3,48,16,128]{3,2,1,0:T(8,128)(2,1)} %bitcast.7, s32[3,16,128]{2,1,0:T(8,128)} %bitcast.9, s32[16,128]{1,0:T(8,128)} %bitcast.10, f32[4]{0:T(128)} %viscosity_hbm.1, f32[16,128]{1,0:T(8,128)} %bitcast.11, bf16[288,256]{1,0:T(8,128)(2,1)} %bitcast.8, bf16[288,256]{1,0:T(8,128)(2,1)} %flux_hbm.1, ...), custom_call_target="tpu_custom_call" | custom-call | tf_op jit(solution)/shard_map/apply/pallas_call | solution.py:444
  18.6 2.1 %copy.11 = bf16[3,48,4,4,128]{4,3,2,1,0:T(4,128)(2,1)} copy(bf16[3,48,4,4,128]{4,3,2,1,0:T(4,128)(2,1)} %bitcast.6) | data formatting | bytes 1179648

commit v3 on v2

--- a/solution.py
+++ b/solution.py
@@ -56,26 +56,18 @@
     return np.concatenate([high, high, low], axis=1)
 
 
-def one_hot(rows):
-    i = lax.broadcasted_iota(jnp.int32, (rows, rows), 0)
-    j = lax.broadcasted_iota(jnp.int32, (rows, rows), 1)
-    hit = jnp.logical_and((i & 15) == (j >> 4), (i >> 4) == (j & 15))
-    return jnp.where(hit, 1.0, 0.0).astype(jnp.bfloat16)
-
-
 def kernel(
     count_x, count_y, wx, wy,
     traces_hbm, dirichlet_hbm, class_hbm, viscosity_hbm, diag_hbm, solve_hbm, flux_hbm, gather_hbm, spread_hbm,
-    out_hbm,
-    traces, dirichlet, classes, viscosity, diag, solve_t, flux_map, gather, spread, result,
-    swap, solve_map, lifted, keep, scale, halo_x, halo_y, first_y, flag_x, flag_y, keep_x, keep_y,
-    residual, high, final, send_x, send_y, recv_x, recv_y,
+    out,
+    traces, dirichlet, classes, viscosity, diag, solve_t, flux_map, gather, spread,
+    staged, solve_map, lifted, keep, scale, halo_x, halo_y, first_y, flag_x, flag_y, keep_x, keep_y,
+    residual, high, send_x, send_y, recv_x, recv_y,
     edge_x, edge_y, edge_c, rim_x, rim_y, rim_c,
-    load_sem, store_sem, send_sem, recv_sem, ready,
+    load_sem, send_sem, recv_sem, ready,
 ):
     columns, depth = wx * wy, traces.shape[3]
     faces = traces.shape[1]
-    groups = faces // 16
     me_x, me_y = lax.axis_index("gx"), lax.axis_index("gy")
     there = {-1: (me_x > 0, me_y > 0), 0: (None, None), 1: (me_x < count_x - 1, me_y < count_y - 1)}
 
@@ -149,21 +141,15 @@
     for exchange in first + [terms_x, terms_y] + rims:
         exchange.clear()
 
-    swap[...] = one_hot(256)
     lane = lax.broadcasted_iota(jnp.int32, (8, depth), 1)
     row = lax.broadcasted_iota(jnp.int32, (8, depth), 0)
     lane_faces = lax.broadcasted_iota(jnp.int32, (faces, depth), 1)
 
-    def to_columns(pairs):
-        moved = jnp.concatenate([traces[d, 16 * g : 16 * g + 16].reshape(256, depth) for d, g in pairs], axis=1)
-        moved = jnp.dot(swap[...], moved, preferred_element_type=jnp.float32)
-        for index, (d, g) in enumerate(pairs):
-            for c in range(columns):
-                piece = moved[16 * c : 16 * c + 16, index * depth : (index + 1) * depth]
-                lifted[d, c, 16 * g : 16 * g + 16] = (piece * keep[d, c : c + 1]).astype(jnp.bfloat16)
-
-    def in_pairs(items):
-        return [items[i : i + 2] for i in range(0, len(items), 2)]
+    def to_columns(d):
+        for n in range(faces):
+            staged[d, n * columns : (n + 1) * columns] = traces[d, n].astype(jnp.float32) * keep[d]
+        for c in range(columns):
+            lifted[d, c] = staged[d, pl.ds(c, faces, stride=columns)].astype(jnp.bfloat16)
 
     loads[0].wait()
     keep[...] = 1.0 - dirichlet[...].astype(jnp.float32)
@@ -172,8 +158,8 @@
         flag_y[x : x + 1] = keep[1, x * wy : x * wy + 1]
     loads[1].wait()
     loads[2].wait()
-    for pair in in_pairs([(d, g) for d in (1, 0) for g in range(groups)]):
-        to_columns(pair)
+    to_columns(1)
+    to_columns(0)
     for x in range(wx):
         first_y[x] = lifted[1, x * wy]
     pl.semaphore_wait(barrier, total)
@@ -186,8 +172,7 @@
             pl.semaphore_signal(ready, inc=1, device_id=device(dx, 0), device_id_type=MESH)
 
     loads[3].wait()
-    for pair in in_pairs([(2, g) for g in range(groups)]):
-        to_columns(pair)
+    to_columns(2)
     for load in loads[4:7]:
         load.wait()
     solve_map[...] = solve_t[...].T
@@ -348,41 +333,34 @@
         upper = value.astype(jnp.bfloat16)
         lower = (value - upper.astype(jnp.float32)).astype(jnp.bfloat16)
         stacks.append(jnp.concatenate([upper, lower, upper], axis=0))
-    stores = []
-    for d in (2, 0, 1):
-        if d == 0:
-            terms_x.arrive()
-        if d == 1:
-            terms_y.arrive()
-        for start in range(0, columns, 4):
-            chosen = range(start, start + 4)
-            lift = jnp.dot(
-                spread[d * faces : (d + 1) * faces],
-                jnp.concatenate([stacks[c] for c in chosen], axis=1),
-                preferred_element_type=jnp.float32,
-            )
-            for index, c in enumerate(chosen):
-                x, y = c // wy, c % wy
+    terms_x.arrive()
+    terms_y.arrive()
+    for start in range(0, columns, 4):
+        chosen = range(start, start + 4)
+        lift = jnp.dot(
+            spread[...], jnp.concatenate([stacks[c] for c in chosen], axis=1), preferred_element_type=jnp.float32
+        )
+        for index, c in enumerate(chosen):
+            x, y = c // wy, c % wy
+            for d in range(3):
                 value = residual[d, c]
                 if d == 0 and x == 0:
                     value = value + recv_x[y].astype(jnp.float32)
                 if d == 1 and y == 0:
                     value = value + recv_y[x].astype(jnp.float32)
-                piece = lift[:, index * depth : (index + 1) * depth]
-                final[d, c] = (value + keep[d, c : c + 1] * piece).astype(jnp.bfloat16)
-        for pair in in_pairs(list(range(groups))):
-            moved = jnp.concatenate(
-                [final[d, :, 16 * g : 16 * g + 16].reshape(256, depth) for g in pair], axis=1
-            )
-            moved = jnp.dot(swap[...], moved, preferred_element_type=jnp.float32).astype(jnp.bfloat16)
-            for index, g in enumerate(pair):
-                piece = moved[:, index * depth : (index + 1) * depth]
-                result[d, 16 * g : 16 * g + 16] = piece.reshape(16, columns, depth)
-        stores.append(pltpu.make_async_copy(result.at[d], out_hbm.at[d], store_sem.at[d]))
-        stores[-1].start()
+                piece = lift[d * faces : (d + 1) * faces, index * depth : (index + 1) * depth]
+                out[d, c * faces : (c + 1) * faces] = value + keep[d, c : c + 1] * piece
 
     for exchange in first + rims + [terms_x, terms_y]:
         exchange.drain()
+
+def deliver(faces, columns, values, out_hbm, rounded, store_sem):
+    stores = []
+    for d in range(3):
+        for n in range(faces):
+            rounded[d, n] = values[d, pl.ds(n, columns, stride=faces)].astype(jnp.bfloat16)
+        stores.append(pltpu.make_async_copy(rounded.at[d], out_hbm.at[d], store_sem.at[d]))
+        stores[-1].start()
     for store in stores:
         store.wait()
 
@@ -409,8 +387,7 @@
     scratch = [
         pltpu.SMEM(a.shape, a.dtype) if index == 3 else pltpu.VMEM(a.shape, a.dtype) for index, a in enumerate(operands)
     ] + [
-        pltpu.VMEM((3, faces, columns, depth), bf16),
-        pltpu.VMEM((256, 256), bf16),
+        pltpu.VMEM((3, faces * columns, depth), f32),
         pltpu.VMEM((inner, 6 * faces), bf16),
         pltpu.VMEM((3, columns, faces, depth), bf16),
         pltpu.VMEM((3, columns, depth), f32),
@@ -424,7 +401,6 @@
         pltpu.VMEM((wx, depth), f32),
         pltpu.VMEM((3, columns, faces, depth), f32),
         pltpu.VMEM((2, columns, faces, depth), f32),
-        pltpu.VMEM((3, columns, faces, depth), bf16),
         pltpu.VMEM((wy, faces, depth), bf16),
         pltpu.VMEM((wx, faces, depth), bf16),
         pltpu.VMEM((wy, faces, depth), bf16),
@@ -436,20 +412,28 @@
         pltpu.VMEM((2, rims_y, 8, depth), f32),
         pltpu.VMEM((2, 2, 8, depth), f32),
         pltpu.SemaphoreType.DMA((len(operands) + 2,)),
-        pltpu.SemaphoreType.DMA((3,)),
         pltpu.SemaphoreType.DMA((exchanges,)),
         pltpu.SemaphoreType.DMA((exchanges,)),
         pltpu.SemaphoreType.REGULAR,
     ]
     result = pl.pallas_call(
         functools.partial(kernel, count_x, count_y, wx, wy),
-        out_shape=jax.ShapeDtypeStruct((3, faces, columns, depth), bf16),
+        out_shape=pltpu.VMEM((3, columns * faces, depth), f32),
         in_specs=[anywhere] * len(operands),
-        out_specs=anywhere,
+        out_specs=pl.BlockSpec(memory_space=pltpu.VMEM),
         scratch_shapes=scratch,
         compiler_params=pltpu.CompilerParams(collective_id=0, has_side_effects=True),
         name="apply",
     )(*operands)
+    result = pl.pallas_call(
+        functools.partial(deliver, faces, columns),
+        out_shape=jax.ShapeDtypeStruct((3, faces, columns, depth), bf16),
+        in_specs=[pl.BlockSpec(memory_space=pltpu.VMEM)],
+        out_specs=anywhere,
+        scratch_shapes=[pltpu.VMEM((3, faces, columns, depth), bf16), pltpu.SemaphoreType.DMA((3,))],
+        compiler_params=pltpu.CompilerParams(vmem_limit_bytes=16 * 2**20),
+        name="deliver",
+    )(result)
     return result.reshape(3, faces, wx, wy, depth)
 
 

time: 20.9 us -> 18.2 us (0.87)
  local copies, waits for them, and re-layouts: 2.08 us -> 0 us
  Pallas kernels: 18.6 us -> 18.1 us
    unnamed x1 -> x0, local copies, waits for them, and re-layouts: 2.08 us -> none
    pallas_call x1, Pallas kernels: 18.6 us -> 17 us  [local(): pl.pallas_call(functools.partial(kernel, count_x, count_y, wx, wy), out_s...]
    pallas_call x0 -> x1, Pallas kernels: none -> 1.05 us  [local(): pl.pallas_call(functools.partial(deliver, faces, columns), out_shape=jax....]
where the time goes in v3:
time: 18.2 us; the launch traced here: 18.1 us
  Pallas kernels  18.1 us (99%)
    pallas_call x1, Pallas kernels, local(): pl.pallas_call(functools.partial(kernel, count_x, count_y, wx, wy), out_s...  17 us
    pallas_call x1, Pallas kernels, local(): pl.pallas_call(functools.partial(deliver, faces, columns), out_shape=jax....  1.05 us

profile of v3, /device:TPU:320, one launch (start us, length us, event | category | flops | bytes accessed | tf_op | source)
XLA Modules:
  0.0 18.1 jit_solution(16769343223499777029)
XLA Ops:
  0.0 17.0 %apply.1.values = f32[3,768,128]{2,1,0:T(8,128)S(1)} custom-call(bf16[3,48,16,128]{3,2,1,0:T(8,128)(2,1)} %bitcast.6, s32[3,16,128]{2,1,0:T(8,128)} %bitcast.8, s32[16,128]{1,0:T(8,128)} %bitcast.9, f32[4]{0:T(128)} %viscosity_hbm.1, f32[16,128]{1,0:T(8,128)} %bitcast.10, bf16[288,256]{1,0:T(8,128)(2,1)} %bitcast.7, bf16[288,256]{1,0:T(8,128)(2,1)} %flux_hbm.1, ...), custom_call_target="tpu_custom_call" | custom-call | tf_op jit(solution)/shard_map/apply/pallas_call | solution.py:419
  17.0 1.0 %deliver.1 = bf16[3,48,16,128]{3,2,1,0:T(8,128)(2,1)} custom-call(f32[3,768,128]{2,1,0:T(8,128)S(1)} %apply.1.values), custom_call_target="tpu_custom_call" | custom-call | tf_op jit(solution)/shard_map/deliver/pallas_call | solution.py:428

commit v4 on v3

--- a/solution.py
+++ b/solution.py
@@ -13,6 +13,7 @@
 
 MESH = pl.DeviceIdType.MESH
 penalty = 0.5
+ORDER = (0, 2, 4, 5, 1, 3)
 CORNER = 4
 
 
@@ -61,8 +62,8 @@
     traces_hbm, dirichlet_hbm, class_hbm, viscosity_hbm, diag_hbm, solve_hbm, flux_hbm, gather_hbm, spread_hbm,
     out,
     traces, dirichlet, classes, viscosity, diag, solve_t, flux_map, gather, spread,
-    staged, solve_map, lifted, keep, scale, halo_x, halo_y, first_y, flag_x, flag_y, keep_x, keep_y,
-    residual, high, send_x, send_y, recv_x, recv_y,
+    staged, product, lifted, keep, scale, visc, halo_x, halo_y, first_y, flag_x, flag_y, keep_x, keep_y,
+    residual, high, base, send_x, send_y, recv_x, recv_y, visc_x, visc_y, prev_x, prev_y, last_x, last_y, corner_x, corner_y,
     edge_x, edge_y, edge_c, rim_x, rim_y, rim_c,
     load_sem, send_sem, recv_sem, ready,
 ):
@@ -128,6 +129,11 @@
     flags_y = Exchange(3, 0, -1, flag_y, keep_y)
     terms_x = Exchange(4, 1, 0, send_x, recv_x)
     terms_y = Exchange(5, 0, 1, send_y, recv_y)
+    class_x = Exchange(6, 1, 0, visc_x, prev_x)
+    class_y = Exchange(7, 0, 1, visc_y, prev_y)
+    final_x = Exchange(8, 1, 0, last_x, corner_x)
+    final_y = Exchange(9, 0, 1, last_y, corner_y)
+    upward = [class_x, class_y, terms_x, terms_y]
     first = [flags_y, traces_y, flags_x, traces_x]
     rims = []
     for slot, (dx, dy) in enumerate(around):
@@ -137,8 +143,8 @@
             source, target = edge_y.at[(dy + 1) // 2], rim_y.at[(dy + 1) // 2]
         else:
             source, target = edge_c.at[(dx + 1) // 2, (dy + 1) // 2], rim_c.at[(dx + 1) // 2, (dy + 1) // 2]
-        rims.append(Exchange(6 + slot, dx, dy, source, target))
-    for exchange in first + [terms_x, terms_y] + rims:
+        rims.append(Exchange(10 + slot, dx, dy, source, target))
+    for exchange in first + upward + [final_x, final_y] + rims:
         exchange.clear()
 
     lane = lax.broadcasted_iota(jnp.int32, (8, depth), 1)
@@ -175,51 +181,73 @@
     to_columns(2)
     for load in loads[4:7]:
         load.wait()
-    solve_map[...] = solve_t[...].T
-    visc = jnp.zeros(classes.shape, jnp.float32)
+    level_sum = jnp.zeros(classes.shape, jnp.float32)
     for level in range(viscosity.shape[0]):
-        visc = visc + jnp.where(classes[...] == level, viscosity[level], 0.0)
+        level_sum = level_sum + jnp.where(classes[...] == level, viscosity[level], 0.0)
+    visc[...] = level_sum
+    visc_x[...] = level_sum[columns - wy :]
+    for x in range(wx):
+        c = x * wy + wy - 1
+        visc_y[x : x + 1] = level_sum[c : c + 1]
+    class_x.start()
+    class_y.start()
     lanes_c = lax.broadcasted_iota(jnp.int32, (columns, depth), 1)
     for d in range(3):
-        scale[2 * d] = visc * keep[d]
-    scale[5] = visc * jnp.where(lanes_c == depth - 1, 0.0, pltpu.roll(keep[2], depth - 1, 1))
-    scale[1, : columns - wy] = visc[: columns - wy] * keep[0, wy:]
-    scale[3, : columns - 1] = visc[: columns - 1] * keep[1, 1:]
+        scale[2 * d] = level_sum * keep[d]
+    scale[5] = level_sum * jnp.where(lanes_c == depth - 1, 0.0, pltpu.roll(keep[2], depth - 1, 1))
+    scale[1, : columns - wy] = level_sum[: columns - wy] * keep[0, wy:]
+    scale[3, : columns - 1] = level_sum[: columns - 1] * keep[1, 1:]
     for load in loads[7:]:
         load.wait()
+    turned = jnp.concatenate([solve_t[f * faces : (f + 1) * faces] for f in ORDER], axis=0).T
+    product[...] = jnp.dot(flux_map[...], turned, preferred_element_type=jnp.float32).astype(jnp.bfloat16)
+
+    known = 4 * faces
+    late = known // 128 * 128
+    filler = jnp.zeros((known - late, depth), jnp.bfloat16)
+    nothing = jnp.zeros((faces, depth), jnp.bfloat16)
+
+    def rows_of(face_slot):
+        return slice(face_slot * faces, (face_slot + 1) * faces)
+
+    def lanes_of(index):
+        return slice(index * depth, (index + 1) * depth)
+
+    def z_above(c):
+        low_z = lifted[2, c].astype(jnp.float32)
+        return jnp.where(lane_faces == depth - 1, 0.0, pltpu.roll(low_z, depth - 1, 1)).astype(jnp.bfloat16)
+
+    def low_part(c):
+        return [lifted[0, c], lifted[1, c], lifted[2, c], z_above(c)]
+
+    def high_x(c):
+        return lifted[0, c + wy] if c + wy < columns else halo_x[c % wy]
+
+    def high_y(c):
+        return lifted[1, c + 1] if c % wy + 1 < wy else halo_y[c // wy]
+
+    def side_by_side(blocks):
+        return jnp.concatenate([jnp.concatenate(block, axis=0) for block in blocks], axis=1)
+
+    def late_dot(left_rows, blocks):
+        return jnp.dot(
+            product[left_rows, late:],
+            side_by_side([[filler, a, b] for a, b in blocks]),
+            preferred_element_type=jnp.float32,
+        )
 
     corners = {}
 
-    def process(chosen, after_terms=lambda: None):
-        pieces = []
-        for c in chosen:
-            x, y = c // wy, c % wy
-            low_z = lifted[2, c].astype(jnp.float32)
-            high_z = jnp.where(lane_faces == depth - 1, 0.0, pltpu.roll(low_z, depth - 1, 1)).astype(jnp.bfloat16)
-            pieces.append(
-                jnp.concatenate(
-                    [
-                        lifted[0, c],
-                        lifted[0, c + wy] if x + 1 < wx else halo_x[y],
-                        lifted[1, c],
-                        lifted[1, c + 1] if y + 1 < wy else halo_y[x],
-                        lifted[2, c],
-                        high_z,
-                    ],
-                    axis=0,
-                )
-            )
-        element = jnp.concatenate(pieces, axis=1)
-        interior = jnp.dot(solve_map[...], element, preferred_element_type=jnp.float32).astype(jnp.bfloat16)
-        flux = jnp.dot(flux_map[...], interior, preferred_element_type=jnp.float32)
+    def finish(chosen, flux, faces_in):
         rounded = []
         for index, c in enumerate(chosen):
             x, y = c // wy, c % wy
-            lanes = slice(index * depth, (index + 1) * depth)
             parts = []
             for face_slot in range(6):
-                rows = slice(face_slot * faces, (face_slot + 1) * faces)
-                term = flux[rows, lanes] + penalty * pieces[index][rows].astype(jnp.float32)
+                term = flux(index, face_slot)
+                trace = faces_in[index][face_slot]
+                if trace is not None:
+                    term = term + penalty * trace.astype(jnp.float32)
                 parts.append(term * scale[face_slot, c : c + 1])
             residual[0, c] = parts[0]
             residual[1, c] = parts[2]
@@ -227,44 +255,77 @@
             cut = jnp.concatenate(parts, axis=0).astype(jnp.bfloat16)
             if x + 1 < wx:
                 high[0, c] = parts[1]
-            else:
-                send_x[y] = cut[faces : 2 * faces]
+            elif y + 1 == wy:
+                last_x[...] = cut[rows_of(1)]
             if y + 1 < wy:
                 high[1, c] = parts[3]
-            else:
-                send_y[x] = cut[3 * faces : 4 * faces]
+            elif x + 1 == wx:
+                last_y[...] = cut[rows_of(3)]
             rounded.append(cut)
-        after_terms()
         both = jnp.dot(gather[...], jnp.concatenate(rounded, axis=1), preferred_element_type=jnp.float32)
         sums = both[:32] + both[32:]
         for index, c in enumerate(chosen):
             x, y = c // wy, c % wy
             for dx, dy in itertools.product(range(2), range(2)):
-                part = sums[16 * dx + 8 * dy : 16 * dx + 8 * dy + 8, index * depth : (index + 1) * depth]
+                part = sums[16 * dx + 8 * dy : 16 * dx + 8 * dy + 8, lanes_of(index)]
                 key = (x + dx, y + dy)
                 corners[key] = part if key not in corners else corners[key] + part
+
+    def process(chosen):
+        slots = [low_part(c) + [high_x(c), high_y(c)] for c in chosen]
+        flux = jnp.dot(product[...], side_by_side(slots), preferred_element_type=jnp.float32)
+        by_slot = [[block[ORDER.index(f)] for f in range(6)] for block in slots]
+        finish(chosen, lambda index, f: flux[rows_of(f), lanes_of(index)], by_slot)
+
+    def prepare(which, chosen):
+        slots = [low_part(c) for c in chosen]
+        flux = jnp.dot(product[:, :known], side_by_side(slots), preferred_element_type=jnp.float32)
+        for index in range(len(chosen)):
+            for f in range(6):
+                term = flux[rows_of(f), lanes_of(index)]
+                if f in ORDER[:4]:
+                    term = term + penalty * slots[index][ORDER.index(f)].astype(jnp.float32)
+                base[which, rows_of(f), lanes_of(index)] = term
+
+    def complete(which, chosen):
+        pairs = [[high_x(c), high_y(c)] for c in chosen]
+        flux = late_dot(slice(None), pairs)
+        by_slot = [[None, a, None, b, None, None] for a, b in pairs]
+        finish(
+            chosen,
+            lambda index, f: base[which, rows_of(f), lanes_of(index)] + flux[rows_of(f), lanes_of(index)],
+            by_slot,
+        )
 
     inner = [c for c in range(columns) if c + wy < columns and c % wy + 1 < wy]
     need_x = [c for c in range(columns) if c + wy >= columns and c % wy + 1 < wy]
     need_y = [c for c in range(columns) if c % wy + 1 == wy]
     early = len(inner) // 4 * 4
+    rim_a, rim_b = need_x + inner[early:], need_y
+    prepare(1, rim_b)
+    prepare(0, rim_a)
+    beside_y = late_dot(rows_of(3), [[high_x(c), nothing] for c in need_y[: wx - 1]])
+    for x, c in enumerate(need_y[: wx - 1]):
+        value = base[1, rows_of(3), lanes_of(x)] + beside_y[:, lanes_of(x)]
+        send_y[x] = (value * visc[c : c + 1]).astype(jnp.bfloat16)
+    beside_x = late_dot(rows_of(1), [[nothing, high_y(c)] for c in need_x])
+    for y, c in enumerate(need_x):
+        value = base[0, rows_of(1), lanes_of(y)] + beside_x[:, lanes_of(y)]
+        send_x[y] = (value * visc[c : c + 1]).astype(jnp.bfloat16)
+    terms_y.start()
+    terms_x.start()
     for start in range(0, early, 4):
         process(inner[start : start + 4])
     flags_x.arrive()
     traces_x.arrive()
     scale[1, columns - wy :] = visc[columns - wy :] * keep_x[...]
-    process(inner[early:] + need_x)
+    complete(0, rim_a)
     flags_y.arrive()
     traces_y.arrive()
     for x in range(wx):
         c = x * wy + wy - 1
         scale[3, c : c + 1] = visc[c : c + 1] * keep_y[x : x + 1]
-
-    def terms_out():
-        terms_y.start()
-        terms_x.start()
-
-    process(need_y, terms_out)
+    complete(1, rim_b)
 
     vertices = list(itertools.product(range(wx + 1), range(wy + 1)))
     for x, y in vertices:
@@ -293,11 +354,65 @@
     for exchange in rims:
         exchange.start()
 
+    final_y.start()
+    final_x.start()
+
     for c in range(columns):
         if c >= wy:
             residual[0, c] += high[0, c - wy]
         if c % wy:
             residual[1, c] += high[1, c - 1]
+    for exchange in upward:
+        exchange.arrive()
+    mine_x = late_dot(rows_of(1), [[lifted[0, y], nothing] for y in range(wy - 1)])
+    for y in range(wy - 1):
+        value = mine_x[:, lanes_of(y)] + penalty * lifted[0, y].astype(jnp.float32)
+        value = value * prev_x[y : y + 1] + recv_x[y].astype(jnp.float32)
+        residual[0, y] += value * keep[0, y : y + 1]
+    mine_y = late_dot(rows_of(3), [[nothing, lifted[1, x * wy]] for x in range(wx - 1)])
+    for x in range(wx - 1):
+        c = x * wy
+        value = mine_y[:, lanes_of(x)] + penalty * lifted[1, c].astype(jnp.float32)
+        value = value * prev_y[x : x + 1] + recv_y[x].astype(jnp.float32)
+        residual[1, c] += value * keep[1, c : c + 1]
+
+    fixes = {}
+
+    def correct(value, inside):
+        below = jnp.broadcast_to(value[CORNER - 1 : CORNER], value.shape)
+        if inside is not None:
+            value = jnp.where(inside, value, 0.0)
+            below = jnp.where(inside, below, 1.0)
+        fix = value / below
+        above = jnp.where(lane == depth - 1, 0.0, pltpu.roll(fix, depth - 1, 1))
+        return jnp.where(row < CORNER, fix, pltpu.roll(above, 4, 0))
+
+    def emit(chosen):
+        stacks = []
+        for c in chosen:
+            x, y = c // wy, c % wy
+            value = jnp.concatenate([fixes[x, y], fixes[x, y + 1], fixes[x + 1, y], fixes[x + 1, y + 1]], axis=0)
+            upper = value.astype(jnp.bfloat16)
+            lower = (value - upper.astype(jnp.float32)).astype(jnp.bfloat16)
+            stacks.append(jnp.concatenate([upper, lower, upper], axis=0))
+        lift = jnp.dot(spread[...], jnp.concatenate(stacks, axis=1), preferred_element_type=jnp.float32)
+        for index, c in enumerate(chosen):
+            x, y = c // wy, c % wy
+            for d in range(3):
+                value = residual[d, c]
+                if d == 0 and x == 0 and y + 1 == wy:
+                    value = value + corner_x[...].astype(jnp.float32)
+                if d == 1 and y == 0 and x + 1 == wx:
+                    value = value + corner_y[...].astype(jnp.float32)
+                piece = lift[d * faces : (d + 1) * faces, lanes_of(index)]
+                out[d, c * faces : (c + 1) * faces] = value + keep[d, c : c + 1] * piece
+
+    for x, y in vertices:
+        if 0 < x < wx and 0 < y < wy:
+            fixes[x, y] = correct(corners[x, y], None)
+    middle = [c for c in range(columns) if 0 < c // wy < wx - 1 and 0 < c % wy < wy - 1]
+    outer = [c for c in range(columns) if c not in middle]
+    emit(middle)
 
     for exchange in rims:
         exchange.arrive()
@@ -306,8 +421,9 @@
         value = source[index // 2]
         return pltpu.roll(value, 4, 0) if index % 2 else value
 
-    fixes = {}
     for x, y in vertices:
+        if (x, y) in fixes:
+            continue
         value = corners[x, y]
         side_x = {0: 0, wx: 1}.get(x)
         side_y = {0: 0, wy: 1}.get(y)
@@ -317,41 +433,13 @@
             value = value + unpack(rim_y.at[1 - side_y], x)
         if side_x is not None and side_y is not None:
             value = value + rim_c[1 - side_x, 1 - side_y]
-        inside = present(int(x == wx), int(y == wy))
-        below = jnp.broadcast_to(value[CORNER - 1 : CORNER], value.shape)
-        if inside is not None:
-            value = jnp.where(inside, value, 0.0)
-            below = jnp.where(inside, below, 1.0)
-        fix = value / below
-        above = jnp.where(lane == depth - 1, 0.0, pltpu.roll(fix, depth - 1, 1))
-        fixes[x, y] = jnp.where(row < CORNER, fix, pltpu.roll(above, 4, 0))
-
-    stacks = []
-    for c in range(columns):
-        x, y = c // wy, c % wy
-        value = jnp.concatenate([fixes[x, y], fixes[x, y + 1], fixes[x + 1, y], fixes[x + 1, y + 1]], axis=0)
-        upper = value.astype(jnp.bfloat16)
-        lower = (value - upper.astype(jnp.float32)).astype(jnp.bfloat16)
-        stacks.append(jnp.concatenate([upper, lower, upper], axis=0))
-    terms_x.arrive()
-    terms_y.arrive()
-    for start in range(0, columns, 4):
-        chosen = range(start, start + 4)
-        lift = jnp.dot(
-            spread[...], jnp.concatenate([stacks[c] for c in chosen], axis=1), preferred_element_type=jnp.float32
-        )
-        for index, c in enumerate(chosen):
-            x, y = c // wy, c % wy
-            for d in range(3):
-                value = residual[d, c]
-                if d == 0 and x == 0:
-                    value = value + recv_x[y].astype(jnp.float32)
-                if d == 1 and y == 0:
-                    value = value + recv_y[x].astype(jnp.float32)
-                piece = lift[d * faces : (d + 1) * faces, index * depth : (index + 1) * depth]
-                out[d, c * faces : (c + 1) * faces] = value + keep[d, c : c + 1] * piece
-
-    for exchange in first + rims + [terms_x, terms_y]:
+        fixes[x, y] = correct(value, present(int(x == wx), int(y == wy)))
+    final_x.arrive()
+    final_y.arrive()
+    for start in range(0, len(outer), 4):
+        emit(outer[start : start + 4])
+
+    for exchange in first + upward + rims + [final_x, final_y]:
         exchange.drain()
 
 def deliver(faces, columns, values, out_hbm, rounded, store_sem):
@@ -368,7 +456,6 @@
 def local(count_x, count_y, traces, dirichlet, visc_class, viscosity, coarse_diag, solve_map, flux_map):
     faces, wx, wy, depth = traces.shape[1:]
     columns = wx * wy
-    inner = solve_map.shape[0]
     operands = (
         traces.reshape(3, faces, columns, depth),
         dirichlet.reshape(3, columns, depth),
@@ -381,17 +468,18 @@
         jnp.asarray(spread_table()),
     )
     anywhere = pl.BlockSpec(memory_space=pl.ANY)
-    exchanges = 14
+    exchanges = 18
     rims_x, rims_y = wy // 2 + 1, wx // 2 + 1
     f32, bf16 = jnp.float32, jnp.bfloat16
     scratch = [
         pltpu.SMEM(a.shape, a.dtype) if index == 3 else pltpu.VMEM(a.shape, a.dtype) for index, a in enumerate(operands)
     ] + [
         pltpu.VMEM((3, faces * columns, depth), f32),
-        pltpu.VMEM((inner, 6 * faces), bf16),
+        pltpu.VMEM((6 * faces, 6 * faces), bf16),
         pltpu.VMEM((3, columns, faces, depth), bf16),
         pltpu.VMEM((3, columns, depth), f32),
         pltpu.VMEM((6, columns, depth), f32),
+        pltpu.VMEM((columns, depth), f32),
         pltpu.VMEM((wy, faces, depth), bf16),
         pltpu.VMEM((wx, faces, depth), bf16),
         pltpu.VMEM((wx, faces, depth), bf16),
@@ -401,10 +489,19 @@
         pltpu.VMEM((wx, depth), f32),
         pltpu.VMEM((3, columns, faces, depth), f32),
         pltpu.VMEM((2, columns, faces, depth), f32),
-        pltpu.VMEM((wy, faces, depth), bf16),
-        pltpu.VMEM((wx, faces, depth), bf16),
-        pltpu.VMEM((wy, faces, depth), bf16),
-        pltpu.VMEM((wx, faces, depth), bf16),
+        pltpu.VMEM((2, 6 * faces, 4 * depth), f32),
+        pltpu.VMEM((wy - 1, faces, depth), bf16),
+        pltpu.VMEM((wx - 1, faces, depth), bf16),
+        pltpu.VMEM((wy - 1, faces, depth), bf16),
+        pltpu.VMEM((wx - 1, faces, depth), bf16),
+        pltpu.VMEM((wy, depth), f32),
+        pltpu.VMEM((wx, depth), f32),
+        pltpu.VMEM((wy, depth), f32),
+        pltpu.VMEM((wx, depth), f32),
+        pltpu.VMEM((faces, depth), bf16),
+        pltpu.VMEM((faces, depth), bf16),
+        pltpu.VMEM((faces, depth), bf16),
+        pltpu.VMEM((faces, depth), bf16),
         pltpu.VMEM((2, rims_x, 8, depth), f32),
         pltpu.VMEM((2, rims_y, 8, depth), f32),
         pltpu.VMEM((2, 2, 8, depth), f32),

time: 18.2 us -> 17.6 us (0.967)
  the two profiles are of different devices: /device:TPU:320 before, /device:TPU:157 now
where the time goes in v4:
time: 17.6 us; the launch traced here: 17.5 us
  Pallas kernels  17.5 us (99%)
    pallas_call x1, Pallas kernels, local(): pl.pallas_call(functools.partial(kernel, count_x, count_y, wx, wy), out_s...  16.4 us
    pallas_call x1, Pallas kernels, local(): pl.pallas_call(functools.partial(deliver, faces, columns), out_shape=jax....  1.05 us

profile of v4, /device:TPU:157, one launch (start us, length us, event | category | flops | bytes accessed | tf_op | source)
XLA Modules:
  0.0 17.5 jit_solution(10671383802330507303)
XLA Ops:
  0.0 16.4 %apply.1.values = f32[3,768,128]{2,1,0:T(8,128)S(1)} custom-call(bf16[3,48,16,128]{3,2,1,0:T(8,128)(2,1)} %bitcast.6, s32[3,16,128]{2,1,0:T(8,128)} %bitcast.8, s32[16,128]{1,0:T(8,128)} %bitcast.9, f32[4]{0:T(128)} %viscosity_hbm.1, f32[16,128]{1,0:T(8,128)} %bitcast.10, bf16[288,256]{1,0:T(8,128)(2,1)} %bitcast.7, bf16[288,256]{1,0:T(8,128)(2,1)} %flux_hbm.1, ...), custom_call_target="tpu_custom_call" | custom-call | tf_op jit(solution)/shard_map/apply/pallas_call | solution.py:516
  16.4 1.0 %deliver.1 = bf16[3,48,16,128]{3,2,1,0:T(8,128)(2,1)} custom-call(f32[3,768,128]{2,1,0:T(8,128)S(1)} %apply.1.values), custom_call_target="tpu_custom_call" | custom-call | tf_op jit(solution)/shard_map/deliver/pallas_call | solution.py:525

commit v5 on v4

v5 whole, which is shorter than its diff:
```python
import functools
import itertools
import math

import jax
import jax.numpy as jnp
import ml_dtypes
import numpy as np
from jax import lax
from jax.experimental import pallas as pl
from jax.experimental.pallas import tpu as pltpu
from jax.sharding import PartitionSpec as P

MESH = pl.DeviceIdType.MESH
penalty = 0.5
ORDER = (0, 2, 4, 5, 1, 3)
CORNER = 4


def corner_table():
    points = [-1.0, -math.sqrt(0.2), math.sqrt(0.2), 1.0]
    table = np.zeros((16, 4), np.float64)
    for a, b, p, q in itertools.product(range(4), range(4), range(2), range(2)):
        table[4 * a + b, 2 * p + q] = (1 + (2 * p - 1) * points[a]) * (1 + (2 * q - 1) * points[b]) / 4
    return table.astype(np.float32)


def in_two(table):
    high = table.astype(ml_dtypes.bfloat16)
    low = (table - high.astype(np.float32)).astype(ml_dtypes.bfloat16)
    return high, low


def gather_table():
    weights = corner_table()
    table = np.zeros((32, 6, 3, 16), np.float32)
    for dx, dy, dz, m in itertools.product(range(2), range(2), range(2), range(3)):
        row = 16 * dx + 8 * dy + CORNER * dz + m
        table[row, dx, m] = weights[:, 2 * dy + dz]
        table[row, 2 + dy, m] = weights[:, 2 * dx + dz]
        table[row, 4 + dz, m] = weights[:, 2 * dx + dy]
    return np.concatenate(in_two(table.reshape(32, 288)), axis=0)


def spread_table():
    weights = corner_table()
    table = np.zeros((3, 3, 16, 32), np.float32)
    for dx, dy, dz, m in itertools.product(range(2), range(2), range(2), range(3)):
        column = 16 * dx + 8 * dy + CORNER * dz + m
        if dx == 0:
            table[0, m, :, column] = weights[:, 2 * dy + dz]
        if dy == 0:
            table[1, m, :, column] = weights[:, 2 * dx + dz]
        if dz == 0:
            table[2, m, :, column] = weights[:, 2 * dx + dy]
    high, low = in_two(table.reshape(144, 32))
    return np.concatenate([high, high, low], axis=1)


AROUND = [(-1, -1), (1, -1), (-1, 1), (1, 1), (0, -1), (0, 1), (-1, 0), (1, 0)]
BELOW = [(-1, -1), (0, -1), (-1, 0)]


def outgoing(wx, wy):
    top_x, top_y = (wx - 1) * wy, wy - 1
    last = wx * wy - 1
    low_x, low_y = [(0, y) for y in range(wy)], [(1, x * wy) for x in range(wx)]
    rim_x, rim_y = [top_x + y for y in range(wy)], [x * wy + top_y for x in range(wx)]
    return {
        (-1, 0): (low_x + [(1, 0)], [top_y], [(3, top_y)]),
        (0, -1): (low_y + [(0, 0)], [top_x], [(1, top_x)]),
        (1, 0): ([(1, top_x)], rim_x, [(1, c) for c in rim_x] + [(3, last)]),
        (0, 1): ([(0, top_y)], rim_y, [(3, c) for c in rim_y] + [(1, last)]),
        (-1, -1): ([(1, 0), (0, 0)], [], []),
        (1, 1): ([], [last], [(1, last), (3, last)]),
        (1, -1): ([(1, top_x)], [top_x], [(1, top_x)]),
        (-1, 1): ([(0, top_y)], [top_y], [(3, top_y)]),
    }


def row_count(faces_out, hexes):
    return -(-(len(faces_out) + 6 * len(hexes)) // 8) * 8


def kernel(
    count_x, count_y, wx, wy,
    traces_hbm, dirichlet_hbm, class_hbm, viscosity_hbm, diag_hbm, solve_hbm, flux_hbm, gather_hbm, spread_hbm,
    out,
    traces, dirichlet, classes, viscosity, diag, solve_t, flux_map, gather, spread,
    staged, product, lifted, keep, scale, visc, residual, high, edge_x, edge_y, edge_c, rim_x, rim_y, rim_c,
    load_sem, send_sem, recv_sem, ready,
    *packs,
):
    columns, depth = wx * wy, traces.shape[3]
    faces = traces.shape[1]
    me_x, me_y = lax.axis_index("gx"), lax.axis_index("gy")
    there = {-1: (me_x > 0, me_y > 0), 0: (None, None), 1: (me_x < count_x - 1, me_y < count_y - 1)}

    def present(dx, dy):
        a, b = there[dx][0], there[dy][1]
        if a is None:
            return b
        return a if b is None else jnp.logical_and(a, b)

    def device(dx, dy):
        return {"gx": me_x + dx, "gy": me_y + dy}

    plan = outgoing(wx, wy)
    barrier = pltpu.get_barrier_semaphore()
    total = 0
    for dx, dy in BELOW:
        total = total + present(dx, dy).astype(jnp.int32)

        @pl.when(present(-dx, -dy))
        def _():
            pl.semaphore_signal(barrier, inc=1, device_id=device(-dx, -dy), device_id_type=MESH)

    loads = [
        (dirichlet_hbm, dirichlet), (traces_hbm.at[0], traces.at[0]), (traces_hbm.at[1], traces.at[1]),
        (viscosity_hbm, viscosity), (class_hbm, classes), (traces_hbm.at[2], traces.at[2]), (solve_hbm, solve_t),
        (flux_hbm, flux_map), (gather_hbm, gather), (diag_hbm, diag), (spread_hbm, spread),
    ]
    loads = [pltpu.make_async_copy(a, b, load_sem.at[i]) for i, (a, b) in enumerate(loads)]
    for load in loads:
        load.start()

    class Exchange:
        def __init__(self, slot, dx, dy, source, target):
            self.to, self.origin, self.target = present(dx, dy), present(-dx, -dy), target
            self.copy = pltpu.make_async_remote_copy(
                src_ref=source, dst_ref=target, send_sem=send_sem.at[slot], recv_sem=recv_sem.at[slot],
                device_id=device(dx, dy), device_id_type=MESH,
            )

        def clear(self):
            @pl.when(jnp.logical_not(self.origin))
            def _():
                self.target[...] = jnp.zeros(self.target.shape, self.target.dtype)

        def start(self):
            pl.when(self.to)(self.copy.start)

        def arrive(self):
            pl.when(self.origin)(self.copy.wait_recv)

        def drain(self):
            pl.when(self.to)(self.copy.wait_send)

    packs = list(packs)
    sent, got, exchanges = {}, {}, {}
    for direction in AROUND:
        for kind, present_here in zip(("trace", "rows", "term"), plan[direction]):
            if kind == "rows":
                present_here = plan[direction][0] + plan[direction][1]
            if present_here:
                sent[kind, direction] = packs.pop(0)
                target = packs.pop(0)
                got[kind, (-direction[0], -direction[1])] = target
                exchanges[kind, direction] = Exchange(len(exchanges), *direction, sent[kind, direction], target)
    for dx, dy in AROUND:
        if dy == 0:
            source, target = edge_x.at[(dx + 1) // 2], rim_x.at[(dx + 1) // 2]
        elif dx == 0:
            source, target = edge_y.at[(dy + 1) // 2], rim_y.at[(dy + 1) // 2]
        else:
            source, target = edge_c.at[(dx + 1) // 2, (dy + 1) // 2], rim_c.at[(dx + 1) // 2, (dy + 1) // 2]
        exchanges["rim", (dx, dy)] = Exchange(len(exchanges), dx, dy, source, target)
    for exchange in exchanges.values():
        exchange.clear()

    def start(kinds, directions):
        for kind in kinds:
            for direction in directions:
                if (kind, direction) in exchanges:
                    exchanges[kind, direction].start()

    def arrive(kind):
        for (name, _), exchange in exchanges.items():
            if name == kind:
                exchange.arrive()

    lane = lax.broadcasted_iota(jnp.int32, (8, depth), 1)
    row = lax.broadcasted_iota(jnp.int32, (8, depth), 0)
    lane_faces = lax.broadcasted_iota(jnp.int32, (faces, depth), 1)

    def to_columns(d):
        for n in range(faces):
            staged[d, n * columns : (n + 1) * columns] = traces[d, n].astype(jnp.float32) * keep[d]
        for c in range(columns):
            lifted[d, c] = staged[d, pl.ds(c, faces, stride=columns)].astype(jnp.bfloat16)

    loads[0].wait()
    keep[...] = 1.0 - dirichlet[...].astype(jnp.float32)
    for load in loads[3:5]:
        load.wait()
    level_sum = jnp.zeros(classes.shape, jnp.float32)
    for level in range(viscosity.shape[0]):
        level_sum = level_sum + jnp.where(classes[...] == level, viscosity[level], 0.0)
    visc[...] = level_sum
    lanes_c = lax.broadcasted_iota(jnp.int32, (columns, depth), 1)
    for d in range(3):
        scale[2 * d] = level_sum * keep[d]
    scale[5] = level_sum * jnp.where(lanes_c == depth - 1, 0.0, pltpu.roll(keep[2], depth - 1, 1))
    scale[1, columns - wy :] = level_sum[columns - wy :]
    scale[1, : columns - wy] = level_sum[: columns - wy] * keep[0, wy:]
    scale[3, : columns - 1] = level_sum[: columns - 1] * keep[1, 1:]
    for x in range(wx):
        c = x * wy + wy - 1
        scale[3, c : c + 1] = visc[c : c + 1]
    for direction, (faces_out, hexes, _) in plan.items():
        target = sent["rows", direction]
        for r, (d, c) in enumerate(faces_out):
            target[r : r + 1] = keep[d, c : c + 1]
        for h, c in enumerate(hexes):
            for f in range(6):
                r = len(faces_out) + 6 * h + f
                target[r : r + 1] = scale[f, c : c + 1]
    loads[1].wait()
    loads[2].wait()
    to_columns(1)
    to_columns(0)
    for direction, (faces_out, _, _) in plan.items():
        for i, (d, c) in enumerate(faces_out):
            sent["trace", direction][i] = lifted[d, c]

    pl.when(total > 0)(lambda: pl.semaphore_wait(barrier, total))
    for slot, (dx, dy) in enumerate(BELOW):

        @pl.when(present(dx, dy))
        def _():
            pl.semaphore_signal(ready.at[slot], inc=1, device_id=device(dx, dy), device_id_type=MESH)

    start(["trace", "rows"], BELOW)
    loads[5].wait()
    to_columns(2)
    for load in loads[6:]:
        load.wait()
    turned = jnp.concatenate([solve_t[f * faces : (f + 1) * faces] for f in ORDER], axis=0).T
    product[...] = jnp.dot(flux_map[...], turned, preferred_element_type=jnp.float32).astype(jnp.bfloat16)

    known = 4 * faces
    late = known // 128 * 128
    filler = jnp.zeros((known - late, depth), jnp.bfloat16)
    nothing = jnp.zeros((faces, depth), jnp.bfloat16)

    def rows_of(face_slot):
        return slice(face_slot * faces, (face_slot + 1) * faces)

    def lanes_of(index):
        return slice(index * depth, (index + 1) * depth)

    def z_above(c):
        low_z = lifted[2, c].astype(jnp.float32)
        return jnp.where(lane_faces == depth - 1, 0.0, pltpu.roll(low_z, depth - 1, 1)).astype(jnp.bfloat16)

    def low_part(c):
        return [lifted[0, c], lifted[1, c], lifted[2, c], z_above(c)]

    def high_x(c):
        return lifted[0, c + wy] if c + wy < columns else nothing

    def high_y(c):
        return lifted[1, c + 1] if c % wy + 1 < wy else nothing

    def side_by_side(blocks):
        return jnp.concatenate([jnp.concatenate(block, axis=0) for block in blocks], axis=1)

    def late_dot(left_rows, blocks):
        return jnp.dot(
            product[left_rows, late:],
            side_by_side([[filler, a, b] for a, b in blocks]),
            preferred_element_type=jnp.float32,
        )

    corners = {}

    def gathered(into, chosen, rounded):
        both = jnp.dot(gather[...], jnp.concatenate(rounded, axis=1), preferred_element_type=jnp.float32)
        sums = both[:32] + both[32:]
        for index, (x, y) in enumerate(chosen):
            for dx, dy in itertools.product(range(2), range(2)):
                key = (x + dx, y + dy)
                if 0 <= key[0] <= wx and 0 <= key[1] <= wy:
                    part = sums[16 * dx + 8 * dy : 16 * dx + 8 * dy + 8, lanes_of(index)]
                    into[key] = part if key not in into else into[key] + part

    def process(chosen):
        slots = [low_part(c) + [high_x(c), high_y(c)] for c in chosen]
        flux = jnp.dot(product[...], side_by_side(slots), preferred_element_type=jnp.float32)
        rounded = []
        for index, c in enumerate(chosen):
            x, y = c // wy, c % wy
            parts = []
            for f in range(6):
                term = flux[rows_of(f), lanes_of(index)]
                term = term + penalty * slots[index][ORDER.index(f)].astype(jnp.float32)
                parts.append(term * scale[f, c : c + 1])
            residual[0, c] = parts[0]
            residual[1, c] = parts[2]
            residual[2, c] = parts[4] + pltpu.roll(parts[5], 1, 1)
            for f, outer_face in ((1, x + 1 == wx), (3, y + 1 == wy)):
                if not outer_face:
                    high[f // 2, c] = parts[f]
                    continue
                sealed = parts[f].astype(jnp.bfloat16)
                for direction in AROUND:
                    if (f, c) in plan[direction][2]:
                        sent["term", direction][plan[direction][2].index((f, c))] = sealed
                parts[f] = jnp.zeros_like(parts[f])
            rounded.append(jnp.concatenate(parts, axis=0).astype(jnp.bfloat16))
        gathered(corners, [(c // wy, c % wy) for c in chosen], rounded)

    def foreign(origin, d, c):
        i = plan[-origin[0], -origin[1]][0].index((d, c))
        return got["trace", origin][i], got["rows", origin][i : i + 1]

    def foreign_scale(origin, c):
        faces_in, hexes, _ = plan[-origin[0], -origin[1]]
        r = len(faces_in) + 6 * hexes.index(c)
        return [got["rows", origin][r + f : r + f + 1] for f in range(6)]

    def foreign_term(origin, f, c):
        return got["term", origin][plan[-origin[0], -origin[1]][2].index((f, c))]

    def own_term(f, c):
        direction = (1, 0) if f == 1 else (0, 1)
        return sent["term", direction][plan[direction][2].index((f, c))]

    top_x, top_y, last = (wx - 1) * wy, wy - 1, columns - 1

    def late_hexes():
        def mine(c):
            return lambda: [scale[f, c : c + 1] for f in range(6)]

        for y in range(wy):
            c = top_x + y
            second = (foreign((0, 1), 1, top_x), own_term(3, c)) if y == top_y else None
            yield (wx - 1, y), (foreign((1, 0), 0, y), own_term(1, c)), second, mine(c)
        for x in range(wx - 1):
            c = x * wy + top_y
            yield (x, top_y), None, (foreign((0, 1), 1, x * wy), own_term(3, c)), mine(c)
        for y in range(wy):
            c = top_x + y
            second = (foreign((-1, 1), 1, top_x), foreign_term((-1, 0), 3, c)) if y == top_y else None
            first = ((lifted[0, y], keep[0, y : y + 1]), foreign_term((-1, 0), 1, c))
            yield (-1, y), first, second, lambda c=c: foreign_scale((-1, 0), c)
        for x in range(wx):
            c = x * wy + top_y
            first = (foreign((1, -1), 0, top_y), foreign_term((0, -1), 1, c)) if x == wx - 1 else None
            second = ((lifted[1, x * wy], keep[1, x * wy : x * wy + 1]), foreign_term((0, -1), 3, c))
            yield (x, -1), first, second, lambda c=c: foreign_scale((0, -1), c)
        yield (
            (-1, -1),
            (foreign((0, -1), 0, top_y), foreign_term((-1, -1), 1, last)),
            (foreign((-1, 0), 1, top_x), foreign_term((-1, -1), 3, last)),
            lambda: foreign_scale((-1, -1), last),
        )
        first = (foreign((0, 1), 0, 0), foreign_term((-1, 1), 1, top_x))
        yield (-1, wy), first, None, lambda: foreign_scale((-1, 1), top_x)
        second = (foreign((1, 0), 1, 0), foreign_term((1, -1), 3, top_y))
        yield (wx, -1), None, second, lambda: foreign_scale((1, -1), top_y)
        second = (foreign((1, 1), 1, 0), foreign_term((1, 0), 3, top_y))
        yield (wx, wy - 1), None, second, lambda: foreign_scale((1, 0), top_y)
        first = (foreign((1, 1), 0, 0), foreign_term((0, 1), 1, top_x))
        yield (wx - 1, wy), first, None, lambda: foreign_scale((0, 1), top_x)

    def act(chosen):
        pairs = [[item[0][0] if item else nothing for item in (first, second)] for _, first, second, _ in chosen]
        flux = late_dot(slice(None), pairs)
        rounded = []
        for index, ((x, y), first, second, scales) in enumerate(chosen):
            scales = scales()
            parts = []
            for f in range(6):
                value = flux[rows_of(f), lanes_of(index)]
                item = {1: first, 3: second}.get(f)
                if item is not None:
                    (trace, flags), term = item
                    value = value + penalty * trace.astype(jnp.float32)
                    value = (value * scales[f] + term.astype(jnp.float32)) * flags
                else:
                    value = value * scales[f]
                parts.append(value)
            if 0 <= x < wx and 0 <= y < wy:
                c = x * wy + y
                residual[0, c] += parts[0]
                residual[1, c] += parts[2]
                residual[2, c] += parts[4] + pltpu.roll(parts[5], 1, 1)
                if x + 1 < wx:
                    residual[0, c + wy] += parts[1]
                if y + 1 < wy:
                    residual[1, c + 1] += parts[3]
            elif x == -1 and 0 <= y < wy:
                residual[0, y] += parts[1]
            elif y == -1 and 0 <= x < wx:
                residual[1, x * wy] += parts[3]
            rounded.append(jnp.concatenate(parts, axis=0).astype(jnp.bfloat16))
        gathered(extra, [item[0] for item in chosen], rounded)

    order = [c for c in range(columns) if c >= top_x] + [c for c in range(columns) if c < top_x and c % wy == top_y]
    order += [c for c in range(columns) if c not in order]
    for start_at in range(0, columns, 4):
        process(order[start_at : start_at + 4])
        if start_at + 4 == 8:
            start(["term"], BELOW)

    vertices = list(itertools.product(range(wx + 1), range(wy + 1)))

    def settle(value):
        above = pltpu.roll(jnp.where(lane == depth - 1, 0.0, value), 1, 1)
        return value + pltpu.roll(above, 4, 0)

    for x, y in vertices:
        value = settle(corners[x, y])
        if x < wx and y < wy:
            corners[x, y] = jnp.where(row == CORNER - 1, diag[x * wy + y : x * wy + y + 1], value)
        else:
            corners[x, y] = jnp.where(row == CORNER - 1, 0.0, value)

    def pack(target, values):
        for i in range(0, len(values), 2):
            value = values[i]
            if i + 1 < len(values):
                value = jnp.where(row < CORNER, value, pltpu.roll(values[i + 1], 4, 0))
            target[i // 2] = value

    for side in range(2):
        for other in range(2):
            edge_c[side, other] = corners[side * wx, other * wy]
    for side in range(2):
        pack(edge_y.at[side], [corners[x, side * wy] for x in range(wx + 1)])
        pack(edge_x.at[side], [corners[side * wx, y] for y in range(wy + 1)])
    start(["rim"], BELOW)
    for slot, directions in ((2, [(1, -1), (1, 0)]), (1, [(-1, 1), (0, 1)]), (0, [(1, 1)])):
        dx, dy = BELOW[slot]
        pl.when(present(-dx, -dy))(lambda: pl.semaphore_wait(ready.at[slot], 1))
        start(["rim", "trace", "rows", "term"], directions)

    for c in range(columns):
        if c >= wy:
            residual[0, c] += high[0, c - wy]
        if c % wy:
            residual[1, c] += high[1, c - 1]
    extra = {}
    arrive("trace")
    arrive("rows")
    arrive("term")
    waiting = list(late_hexes())
    for start_at in range(0, len(waiting), 4):
        act(waiting[start_at : start_at + 4])
    for x, y in vertices:
        if (x, y) in extra:
            corners[x, y] = corners[x, y] + jnp.where(row == CORNER - 1, 0.0, settle(extra[x, y]))

    fixes = {}

    def correct(value, inside):
        below = jnp.broadcast_to(value[CORNER - 1 : CORNER], value.shape)
        if inside is not None:
            value = jnp.where(inside, value, 0.0)
            below = jnp.where(inside, below, 1.0)
        fix = value / below
        above = jnp.where(lane == depth - 1, 0.0, pltpu.roll(fix, depth - 1, 1))
        return jnp.where(row < CORNER, fix, pltpu.roll(above, 4, 0))

    def emit(chosen):
        stacks = []
        for c in chosen:
            x, y = c // wy, c % wy
            value = jnp.concatenate([fixes[x, y], fixes[x, y + 1], fixes[x + 1, y], fixes[x + 1, y + 1]], axis=0)
            upper = value.astype(jnp.bfloat16)
            lower = (value - upper.astype(jnp.float32)).astype(jnp.bfloat16)
            stacks.append(jnp.concatenate([upper, lower, upper], axis=0))
        lift = jnp.dot(spread[...], jnp.concatenate(stacks, axis=1), preferred_element_type=jnp.float32)
        for index, c in enumerate(chosen):
            x, y = c // wy, c % wy
            for d in range(3):
                piece = lift[d * faces : (d + 1) * faces, lanes_of(index)]
                out[d, c * faces : (c + 1) * faces] = residual[d, c] + keep[d, c : c + 1] * piece

    for x, y in vertices:
        if 0 < x < wx and 0 < y < wy:
            fixes[x, y] = correct(corners[x, y], None)
    middle = [c for c in range(columns) if 0 < c // wy < wx - 1 and 0 < c % wy < wy - 1]
    outer = [c for c in range(columns) if c not in middle]
    emit(middle)
    arrive("rim")

    def unpack(source, index):
        value = source[index // 2]
        return pltpu.roll(value, 4, 0) if index % 2 else value

    for x, y in vertices:
        if (x, y) in fixes:
            continue
        value = corners[x, y]
        side_x = {0: 0, wx: 1}.get(x)
        side_y = {0: 0, wy: 1}.get(y)
        if side_x is not None:
            value = value + unpack(rim_x.at[1 - side_x], y)
        if side_y is not None:
            value = value + unpack(rim_y.at[1 - side_y], x)
        if side_x is not None and side_y is not None:
            value = value + rim_c[1 - side_x, 1 - side_y]
        fixes[x, y] = correct(value, present(int(x == wx), int(y == wy)))
    for first_one in range(0, len(outer), 4):
        emit(outer[first_one : first_one + 4])

    for exchange in exchanges.values():
        exchange.drain()


def deliver(faces, columns, values, out_hbm, rounded, store_sem):
    stores = []
    for d in range(3):
        for n in range(faces):
            rounded[d, n] = values[d, pl.ds(n, columns, stride=faces)].astype(jnp.bfloat16)
        stores.append(pltpu.make_async_copy(rounded.at[d], out_hbm.at[d], store_sem.at[d]))
        stores[-1].start()
    for store in stores:
        store.wait()


def local(count_x, count_y, traces, dirichlet, visc_class, viscosity, coarse_diag, solve_map, flux_map):
    faces, wx, wy, depth = traces.shape[1:]
    columns = wx * wy
    operands = (
        traces.reshape(3, faces, columns, depth),
        dirichlet.reshape(3, columns, depth),
        visc_class.reshape(columns, depth),
        viscosity,
        coarse_diag.reshape(columns, depth),
        solve_map.T,
        flux_map,
        jnp.asarray(gather_table()),
        jnp.asarray(spread_table()),
    )
    anywhere = pl.BlockSpec(memory_space=pl.ANY)
    plan = outgoing(wx, wy)
    packs = []
    for direction in AROUND:
        faces_out, hexes, terms = plan[direction]
        shapes = [((len(faces_out), faces, depth), jnp.bfloat16)] if faces_out else []
        shapes.append(((row_count(faces_out, hexes), depth), jnp.float32))
        shapes += [((len(terms), faces, depth), jnp.bfloat16)] if terms else []
        packs += [pltpu.VMEM(*shape) for shape in shapes for _ in range(2)]
    exchanges = len(packs) // 2 + len(AROUND)
    rims_x, rims_y = wy // 2 + 1, wx // 2 + 1
    f32, bf16 = jnp.float32, jnp.bfloat16
    scratch = [
        pltpu.SMEM(a.shape, a.dtype) if index == 3 else pltpu.VMEM(a.shape, a.dtype) for index, a in enumerate(operands)
    ] + [
        pltpu.VMEM((3, faces * columns, depth), f32),
        pltpu.VMEM((6 * faces, 6 * faces), bf16),
        pltpu.VMEM((3, columns, faces, depth), bf16),
        pltpu.VMEM((3, columns, depth), f32),
        pltpu.VMEM((6, columns, depth), f32),
        pltpu.VMEM((columns, depth), f32),
        pltpu.VMEM((3, columns, faces, depth), f32),
        pltpu.VMEM((2, columns, faces, depth), f32),
        pltpu.VMEM((2, rims_x, 8, depth), f32),
        pltpu.VMEM((2, rims_y, 8, depth), f32),
        pltpu.VMEM((2, 2, 8, depth), f32),
        pltpu.VMEM((2, rims_x, 8, depth), f32),
        pltpu.VMEM((2, rims_y, 8, depth), f32),
        pltpu.VMEM((2, 2, 8, depth), f32),
        pltpu.SemaphoreType.DMA((len(operands) + 2,)),
        pltpu.SemaphoreType.DMA((exchanges,)),
        pltpu.SemaphoreType.DMA((exchanges,)),
        pltpu.SemaphoreType.REGULAR((3,)),
    ] + packs
    result = pl.pallas_call(
        functools.partial(kernel, count_x, count_y, wx, wy),
        out_shape=pltpu.VMEM((3, columns * faces, depth), f32),
        in_specs=[anywhere] * len(operands),
        out_specs=pl.BlockSpec(memory_space=pltpu.VMEM),
        scratch_shapes=scratch,
        compiler_params=pltpu.CompilerParams(collective_id=0, has_side_effects=True),
        name="apply",
    )(*operands)
    result = pl.pallas_call(
        functools.partial(deliver, faces, columns),
        out_shape=jax.ShapeDtypeStruct((3, faces, columns, depth), bf16),
        in_specs=[pl.BlockSpec(memory_space=pltpu.VMEM)],
        out_specs=anywhere,
        scratch_shapes=[pltpu.VMEM((3, faces, columns, depth), bf16), pltpu.SemaphoreType.DMA((3,))],
        compiler_params=pltpu.CompilerParams(vmem_limit_bytes=16 * 2**20),
        name="deliver",
    )(result)
    return result.reshape(3, faces, wx, wy, depth)


def solution(mesh):
    count_x, count_y = mesh.shape["gx"], mesh.shape["gy"]
    in_specs = (
        P(None, None, "gx", "gy", None),
        P(None, "gx", "gy", None),
        P("gx", "gy", None),
        P(),
        P("gx", "gy", None),
        P(),
        P(),
    )
    out_specs = P(None, None, "gx", "gy", None)
    return jax.shard_map(
        functools.partial(local, count_x, count_y), mesh=mesh, in_specs=in_specs, out_specs=out_specs, check_vma=False
    )
```

time: 17.6 us -> 21.5 us (1.22)
  the two profiles are of different devices: /device:TPU:157 before, /device:TPU:385 now
where the time goes in v5:
time: 21.5 us; the launch traced here: 21.4 us
  Pallas kernels  21.4 us (100%)
    pallas_call x1, Pallas kernels, local(): pl.pallas_call(functools.partial(kernel, count_x, count_y, wx, wy), out_s...  20.3 us
    pallas_call x1, Pallas kernels, local(): pl.pallas_call(functools.partial(deliver, faces, columns), out_shape=jax....  1.05 us

profile of v5, /device:TPU:385, one launch (start us, length us, event | category | flops | bytes accessed | tf_op | source)
XLA Modules:
  0.0 21.4 jit_solution(18242664362480881807)
XLA Ops:
  0.0 20.3 %apply.1.values = f32[3,768,128]{2,1,0:T(8,128)S(1)} custom-call(bf16[3,48,16,128]{3,2,1,0:T(8,128)(2,1)} %bitcast.6, s32[3,16,128]{2,1,0:T(8,128)} %bitcast.8, s32[16,128]{1,0:T(8,128)} %bitcast.9, f32[4]{0:T(128)} %viscosity_hbm.1, f32[16,128]{1,0:T(8,128)} %bitcast.10, bf16[288,256]{1,0:T(8,128)(2,1)} %bitcast.7, bf16[288,256]{1,0:T(8,128)(2,1)} %flux_hbm.1, ...), custom_call_target="tpu_custom_call" | custom-call | tf_op jit(solution)/shard_map/apply/pallas_call | solution.py:572
  20.3 1.0 %deliver.1 = bf16[3,48,16,128]{3,2,1,0:T(8,128)(2,1)} custom-call(f32[3,768,128]{2,1,0:T(8,128)S(1)} %apply.1.values), custom_call_target="tpu_custom_call" | custom-call | tf_op jit(solution)/shard_map/deliver/pallas_call | solution.py:581

commit v6 on v4

--- a/solution.py
+++ b/solution.py
@@ -81,25 +81,26 @@
     def device(dx, dy):
         return {"gx": me_x + dx, "gy": me_y + dy}
 
-    around = [(-1, -1), (1, -1), (-1, 1), (1, 1), (0, -1), (0, 1), (-1, 0), (1, 0)]
-    barrier = pltpu.get_barrier_semaphore()
-    total = 0
-    for dx, dy in around[4:]:
-        here = present(dx, dy)
-        total = total + here.astype(jnp.int32)
-
-        @pl.when(here)
-        def _():
-            pl.semaphore_signal(barrier, inc=1, device_id=device(dx, dy), device_id_type=MESH)
-
-    loads = [
-        (dirichlet_hbm, dirichlet), (traces_hbm.at[0], traces.at[0]), (traces_hbm.at[1], traces.at[1]),
+    around = [(-1, -1), (0, -1), (-1, 0), (1, -1), (1, 0), (-1, 1), (0, 1), (1, 1)]
+    names = ("dirichlet", "y", "x", "z", "viscosity", "classes", "solve", "flux", "gather", "diag", "spread")
+    pairs = [
+        (dirichlet_hbm, dirichlet), (traces_hbm.at[1], traces.at[1]), (traces_hbm.at[0], traces.at[0]),
         (traces_hbm.at[2], traces.at[2]), (viscosity_hbm, viscosity), (class_hbm, classes), (solve_hbm, solve_t),
         (flux_hbm, flux_map), (gather_hbm, gather), (diag_hbm, diag), (spread_hbm, spread),
     ]
-    loads = [pltpu.make_async_copy(a, b, load_sem.at[i]) for i, (a, b) in enumerate(loads)]
-    for load in loads:
+    loads = {name: pltpu.make_async_copy(a, b, load_sem.at[i]) for i, (name, (a, b)) in enumerate(zip(names, pairs))}
+    for load in loads.values():
         load.start()
+
+    barrier = pltpu.get_barrier_semaphore()
+    total = 0
+    below = [None, (0, -1), (-1, 0)]
+    for dx, dy in below[1:]:
+        total = total + present(dx, dy).astype(jnp.int32)
+
+        @pl.when(present(-dx, -dy))
+        def _():
+            pl.semaphore_signal(barrier, inc=1, device_id=device(-dx, -dy), device_id_type=MESH)
 
     class Exchange:
         def __init__(self, slot, dx, dy, source, target):
@@ -144,43 +145,56 @@
         else:
             source, target = edge_c.at[(dx + 1) // 2, (dy + 1) // 2], rim_c.at[(dx + 1) // 2, (dy + 1) // 2]
         rims.append(Exchange(10 + slot, dx, dy, source, target))
-    for exchange in first + upward + [final_x, final_y] + rims:
-        exchange.clear()
 
     lane = lax.broadcasted_iota(jnp.int32, (8, depth), 1)
     row = lax.broadcasted_iota(jnp.int32, (8, depth), 0)
     lane_faces = lax.broadcasted_iota(jnp.int32, (faces, depth), 1)
 
-    def to_columns(d):
+    def stage(d):
         for n in range(faces):
             staged[d, n * columns : (n + 1) * columns] = traces[d, n].astype(jnp.float32) * keep[d]
-        for c in range(columns):
+
+    def to_columns(d, chosen):
+        for c in chosen:
             lifted[d, c] = staged[d, pl.ds(c, faces, stride=columns)].astype(jnp.bfloat16)
 
-    loads[0].wait()
+    loads["dirichlet"].wait()
     keep[...] = 1.0 - dirichlet[...].astype(jnp.float32)
-    flag_x[...] = keep[0, :wy]
     for x in range(wx):
         flag_y[x : x + 1] = keep[1, x * wy : x * wy + 1]
-    loads[1].wait()
-    loads[2].wait()
-    to_columns(1)
-    to_columns(0)
+    flag_x[...] = keep[0, :wy]
+    loads["y"].wait()
+    stage(1)
     for x in range(wx):
-        first_y[x] = lifted[1, x * wy]
-    pl.semaphore_wait(barrier, total)
-    for exchange in first:
-        exchange.start()
-    for dx in (-1, 1):
-
-        @pl.when(present(dx, 0))
+        first_y[x] = staged[1, pl.ds(x * wy, faces, stride=columns)].astype(jnp.bfloat16)
+    pl.when(total > 0)(lambda: pl.semaphore_wait(barrier, total))
+    def tell(slot, dx, dy, if_present):
+        @pl.when(if_present)
         def _():
-            pl.semaphore_signal(ready, inc=1, device_id=device(dx, 0), device_id_type=MESH)
-
-    loads[3].wait()
-    to_columns(2)
-    for load in loads[4:7]:
-        load.wait()
+            pl.semaphore_signal(ready.at[slot], inc=1, device_id=device(dx, dy), device_id_type=MESH)
+
+    for slot in (1, 2):
+        tell(slot, *below[slot], present(*below[slot]))
+    flags_y.start()
+    traces_y.start()
+    flags_x.start()
+    loads["x"].wait()
+    stage(0)
+    to_columns(0, range(wy))
+    traces_x.start()
+
+    def hear(slot, dx, dy):
+        pl.when(present(dx, dy))(lambda: pl.semaphore_wait(ready.at[slot], 1))
+
+    loads["z"].wait()
+    stage(2)
+    to_columns(0, range(wy, columns))
+    to_columns(1, range(columns))
+    to_columns(2, range(columns))
+    for exchange in first + upward + [final_x, final_y] + rims:
+        exchange.clear()
+    for name in names[4:7]:
+        loads[name].wait()
     level_sum = jnp.zeros(classes.shape, jnp.float32)
     for level in range(viscosity.shape[0]):
         level_sum = level_sum + jnp.where(classes[...] == level, viscosity[level], 0.0)
@@ -189,16 +203,14 @@
     for x in range(wx):
         c = x * wy + wy - 1
         visc_y[x : x + 1] = level_sum[c : c + 1]
-    class_x.start()
-    class_y.start()
     lanes_c = lax.broadcasted_iota(jnp.int32, (columns, depth), 1)
     for d in range(3):
         scale[2 * d] = level_sum * keep[d]
     scale[5] = level_sum * jnp.where(lanes_c == depth - 1, 0.0, pltpu.roll(keep[2], depth - 1, 1))
     scale[1, : columns - wy] = level_sum[: columns - wy] * keep[0, wy:]
     scale[3, : columns - 1] = level_sum[: columns - 1] * keep[1, 1:]
-    for load in loads[7:]:
-        load.wait()
+    for name in names[7:]:
+        loads[name].wait()
     turned = jnp.concatenate([solve_t[f * faces : (f + 1) * faces] for f in ORDER], axis=0).T
     product[...] = jnp.dot(flux_map[...], turned, preferred_element_type=jnp.float32).astype(jnp.bfloat16)
 
@@ -312,10 +324,16 @@
     for y, c in enumerate(need_x):
         value = base[0, rows_of(1), lanes_of(y)] + beside_x[:, lanes_of(y)]
         send_x[y] = (value * visc[c : c + 1]).astype(jnp.bfloat16)
-    terms_y.start()
-    terms_x.start()
     for start in range(0, early, 4):
         process(inner[start : start + 4])
+    hear(2, 1, 0)
+    tell(3, 1, 0, present(1, -1))
+    class_x.start()
+    terms_x.start()
+    hear(1, 0, 1)
+    tell(0, -1, 0, present(-1, 1))
+    class_y.start()
+    terms_y.start()
     flags_x.arrive()
     traces_x.arrive()
     scale[1, columns - wy :] = visc[columns - wy :] * keep_x[...]
@@ -350,12 +368,14 @@
     for side in range(2):
         pack(edge_y.at[side], [corners[x, side * wy] for x in range(wx + 1)])
         pack(edge_x.at[side], [corners[side * wx, y] for y in range(wy + 1)])
-    pl.semaphore_wait(ready, there[-1][0].astype(jnp.int32) + there[1][0].astype(jnp.int32))
-    for exchange in rims:
+    for exchange in rims[1:-1]:
         exchange.start()
-
     final_y.start()
     final_x.start()
+    hear(3, -1, -1)
+    rims[0].start()
+    hear(0, 1, 1)
+    rims[-1].start()
 
     for c in range(columns):
         if c >= wy:
@@ -379,11 +399,11 @@
     fixes = {}
 
     def correct(value, inside):
-        below = jnp.broadcast_to(value[CORNER - 1 : CORNER], value.shape)
+        under = jnp.broadcast_to(value[CORNER - 1 : CORNER], value.shape)
         if inside is not None:
             value = jnp.where(inside, value, 0.0)
-            below = jnp.where(inside, below, 1.0)
-        fix = value / below
+            under = jnp.where(inside, under, 1.0)
+        fix = value / under
         above = jnp.where(lane == depth - 1, 0.0, pltpu.roll(fix, depth - 1, 1))
         return jnp.where(row < CORNER, fix, pltpu.roll(above, 4, 0))
 
@@ -413,6 +433,8 @@
     middle = [c for c in range(columns) if 0 < c // wy < wx - 1 and 0 < c % wy < wy - 1]
     outer = [c for c in range(columns) if c not in middle]
     emit(middle)
+    for exchange in first + upward:
+        exchange.drain()
 
     for exchange in rims:
         exchange.arrive()
@@ -439,7 +461,7 @@
     for start in range(0, len(outer), 4):
         emit(outer[start : start + 4])
 
-    for exchange in first + upward + rims + [final_x, final_y]:
+    for exchange in rims + [final_x, final_y]:
         exchange.drain()
 
 def deliver(faces, columns, values, out_hbm, rounded, store_sem):
@@ -511,7 +533,7 @@
         pltpu.SemaphoreType.DMA((len(operands) + 2,)),
         pltpu.SemaphoreType.DMA((exchanges,)),
         pltpu.SemaphoreType.DMA((exchanges,)),
-        pltpu.SemaphoreType.REGULAR,
+        pltpu.SemaphoreType.REGULAR((4,)),
     ]
     result = pl.pallas_call(
         functools.partial(kernel, count_x, count_y, wx, wy),

time: 17.6 us -> 17.3 us (0.983)
  the two profiles are of different devices: /device:TPU:157 before, /device:TPU:409 now
where the time goes in v6:
time: 17.3 us; the launch traced here: 17.2 us
  Pallas kernels  17.2 us (99%)
    pallas_call x1, Pallas kernels, local(): pl.pallas_call(functools.partial(kernel, count_x, count_y, wx, wy), out_s...  16.1 us
    pallas_call x1, Pallas kernels, local(): pl.pallas_call(functools.partial(deliver, faces, columns), out_shape=jax....  1.05 us

profile of v6, /device:TPU:409, one launch (start us, length us, event | category | flops | bytes accessed | tf_op | source)
XLA Modules:
  0.0 17.2 jit_solution(15429367345431019482)
XLA Ops:
  0.0 16.1 %apply.1.values = f32[3,768,128]{2,1,0:T(8,128)S(1)} custom-call(bf16[3,48,16,128]{3,2,1,0:T(8,128)(2,1)} %bitcast.6, s32[3,16,128]{2,1,0:T(8,128)} %bitcast.8, s32[16,128]{1,0:T(8,128)} %bitcast.9, f32[4]{0:T(128)} %viscosity_hbm.1, f32[16,128]{1,0:T(8,128)} %bitcast.10, bf16[288,256]{1,0:T(8,128)(2,1)} %bitcast.7, bf16[288,256]{1,0:T(8,128)(2,1)} %flux_hbm.1, ...), custom_call_target="tpu_custom_call" | custom-call | tf_op jit(solution)/shard_map/apply/pallas_call | solution.py:538
  16.1 1.0 %deliver.1 = bf16[3,48,16,128]{3,2,1,0:T(8,128)(2,1)} custom-call(f32[3,768,128]{2,1,0:T(8,128)S(1)} %apply.1.values), custom_call_target="tpu_custom_call" | custom-call | tf_op jit(solution)/shard_map/deliver/pallas_call | solution.py:547

commit v7 on v6

--- a/solution.py
+++ b/solution.py
@@ -14,6 +14,8 @@
 MESH = pl.DeviceIdType.MESH
 penalty = 0.5
 ORDER = (0, 2, 4, 5, 1, 3)
+PITCH = 52
+STAGE = 20
 CORNER = 4
 
 
@@ -152,11 +154,11 @@
 
     def stage(d):
         for n in range(faces):
-            staged[d, n * columns : (n + 1) * columns] = traces[d, n].astype(jnp.float32) * keep[d]
+            staged[d, n * STAGE : n * STAGE + columns] = traces[d, n].astype(jnp.float32) * keep[d]
 
     def to_columns(d, chosen):
         for c in chosen:
-            lifted[d, c] = staged[d, pl.ds(c, faces, stride=columns)].astype(jnp.bfloat16)
+            lifted[d, c] = staged[d, pl.ds(c, faces, stride=STAGE)].astype(jnp.bfloat16)
 
     loads["dirichlet"].wait()
     keep[...] = 1.0 - dirichlet[...].astype(jnp.float32)
@@ -166,7 +168,7 @@
     loads["y"].wait()
     stage(1)
     for x in range(wx):
-        first_y[x] = staged[1, pl.ds(x * wy, faces, stride=columns)].astype(jnp.bfloat16)
+        first_y[x] = staged[1, pl.ds(x * wy, faces, stride=STAGE)].astype(jnp.bfloat16)
     pl.when(total > 0)(lambda: pl.semaphore_wait(barrier, total))
     def tell(slot, dx, dy, if_present):
         @pl.when(if_present)
@@ -425,7 +427,7 @@
                 if d == 1 and y == 0 and x + 1 == wx:
                     value = value + corner_y[...].astype(jnp.float32)
                 piece = lift[d * faces : (d + 1) * faces, lanes_of(index)]
-                out[d, c * faces : (c + 1) * faces] = value + keep[d, c : c + 1] * piece
+                out[d, c * PITCH : c * PITCH + faces] = value + keep[d, c : c + 1] * piece
 
     for x, y in vertices:
         if 0 < x < wx and 0 < y < wy:
@@ -433,7 +435,7 @@
     middle = [c for c in range(columns) if 0 < c // wy < wx - 1 and 0 < c % wy < wy - 1]
     outer = [c for c in range(columns) if c not in middle]
     emit(middle)
-    for exchange in first + upward:
+    for exchange in first + upward + rims + [final_x, final_y]:
         exchange.drain()
 
     for exchange in rims:
@@ -461,14 +463,12 @@
     for start in range(0, len(outer), 4):
         emit(outer[start : start + 4])
 
-    for exchange in rims + [final_x, final_y]:
-        exchange.drain()
 
 def deliver(faces, columns, values, out_hbm, rounded, store_sem):
     stores = []
     for d in range(3):
         for n in range(faces):
-            rounded[d, n] = values[d, pl.ds(n, columns, stride=faces)].astype(jnp.bfloat16)
+            rounded[d, n] = values[d, pl.ds(n, columns, stride=PITCH)].astype(jnp.bfloat16)
         stores.append(pltpu.make_async_copy(rounded.at[d], out_hbm.at[d], store_sem.at[d]))
         stores[-1].start()
     for store in stores:
@@ -496,7 +496,7 @@
     scratch = [
         pltpu.SMEM(a.shape, a.dtype) if index == 3 else pltpu.VMEM(a.shape, a.dtype) for index, a in enumerate(operands)
     ] + [
-        pltpu.VMEM((3, faces * columns, depth), f32),
+        pltpu.VMEM((3, (faces + 1) * STAGE, depth), f32),
         pltpu.VMEM((6 * faces, 6 * faces), bf16),
         pltpu.VMEM((3, columns, faces, depth), bf16),
         pltpu.VMEM((3, columns, depth), f32),
@@ -537,7 +537,7 @@
     ]
     result = pl.pallas_call(
         functools.partial(kernel, count_x, count_y, wx, wy),
-        out_shape=pltpu.VMEM((3, columns * faces, depth), f32),
+        out_shape=pltpu.VMEM((3, (columns + 1) * PITCH, depth), f32),
         in_specs=[anywhere] * len(operands),
         out_specs=pl.BlockSpec(memory_space=pltpu.VMEM),
         scratch_shapes=scratch,

time: 17.3 us -> 17.1 us (0.988)
  Pallas kernels: 17.2 us -> 17 us
    pallas_call x1, Pallas kernels: 1.05 us -> 0.85 us  [local(): pl.pallas_call(functools.partial(deliver, faces, columns), out_shape=jax....]
where the time goes in v7:
time: 17.1 us; the launch traced here: 17 us
  Pallas kernels  17 us (99%)
    pallas_call x1, Pallas kernels, local(): pl.pallas_call(functools.partial(kernel, count_x, count_y, wx, wy), out_s...  16.1 us
    pallas_call x1, Pallas kernels, local(): pl.pallas_call(functools.partial(deliver, faces, columns), out_shape=jax....  0.85 us

profile of v7, /device:TPU:409, one launch (start us, length us, event | category | flops | bytes accessed | tf_op | source)
XLA Modules:
  0.0 17.0 jit_solution(14934383862316219467)
XLA Ops:
  0.0 16.1 %apply.1.values = f32[3,884,128]{2,1,0:T(8,128)S(1)} custom-call(bf16[3,48,16,128]{3,2,1,0:T(8,128)(2,1)} %bitcast.6, s32[3,16,128]{2,1,0:T(8,128)} %bitcast.8, s32[16,128]{1,0:T(8,128)} %bitcast.9, f32[4]{0:T(128)} %viscosity_hbm.1, f32[16,128]{1,0:T(8,128)} %bitcast.10, bf16[288,256]{1,0:T(8,128)(2,1)} %bitcast.7, bf16[288,256]{1,0:T(8,128)(2,1)} %flux_hbm.1, ...), custom_call_target="tpu_custom_call" | custom-call | tf_op jit(solution)/shard_map/apply/pallas_call | solution.py:538
  16.1 0.9 %deliver.1 = bf16[3,48,16,128]{3,2,1,0:T(8,128)(2,1)} custom-call(f32[3,884,128]{2,1,0:T(8,128)S(1)} %apply.1.values), custom_call_target="tpu_custom_call" | custom-call | tf_op jit(solution)/shard_map/deliver/pallas_call | solution.py:547

commit v8 on v7

--- a/solution.py
+++ b/solution.py
@@ -340,44 +340,55 @@
     traces_x.arrive()
     scale[1, columns - wy :] = visc[columns - wy :] * keep_x[...]
     complete(0, rim_a)
+    vertices = list(itertools.product(range(wx + 1), range(wy + 1)))
+
+    def settle(chosen):
+        for x, y in chosen:
+            value = corners[x, y]
+            above = pltpu.roll(jnp.where(lane == depth - 1, 0.0, value), 1, 1)
+            value = value + pltpu.roll(above, 4, 0)
+            if x < wx and y < wy:
+                corners[x, y] = jnp.where(row == CORNER - 1, diag[x * wy + y : x * wy + y + 1], value)
+            else:
+                corners[x, y] = jnp.where(row == CORNER - 1, 0.0, value)
+
+    def pack(target, values):
+        for i in range(0, len(values), 2):
+            value = values[i]
+            if i + 1 < len(values):
+                value = jnp.where(row < CORNER, value, pltpu.roll(values[i + 1], 4, 0))
+            target[i // 2] = value
+
+    def pack_y(side):
+        pack(edge_y.at[side], [corners[x, side * wy] for x in range(wx + 1)])
+        for other in range(2):
+            edge_c[other, side] = corners[other * wx, side * wy]
+
+    rim = dict(zip(around, rims))
+    settle([place for place in vertices if place[1] < wy - 1])
+    pack_y(0)
+    rim[0, -1].start()
+    rim[1, -1].start()
+    hear(3, -1, -1)
+    rim[-1, -1].start()
     flags_y.arrive()
     traces_y.arrive()
     for x in range(wx):
         c = x * wy + wy - 1
         scale[3, c : c + 1] = visc[c : c + 1] * keep_y[x : x + 1]
     complete(1, rim_b)
-
-    vertices = list(itertools.product(range(wx + 1), range(wy + 1)))
-    for x, y in vertices:
-        value = corners[x, y]
-        above = pltpu.roll(jnp.where(lane == depth - 1, 0.0, value), 1, 1)
-        value = value + pltpu.roll(above, 4, 0)
-        if x < wx and y < wy:
-            corners[x, y] = jnp.where(row == CORNER - 1, diag[x * wy + y : x * wy + y + 1], value)
-        else:
-            corners[x, y] = jnp.where(row == CORNER - 1, 0.0, value)
-
-    def pack(target, values):
-        for i in range(0, len(values), 2):
-            value = values[i]
-            if i + 1 < len(values):
-                value = jnp.where(row < CORNER, value, pltpu.roll(values[i + 1], 4, 0))
-            target[i // 2] = value
-
+    settle([place for place in vertices if place[1] >= wy - 1])
+    pack_y(1)
+    rim[0, 1].start()
+    rim[-1, 1].start()
     for side in range(2):
-        for other in range(2):
-            edge_c[side, other] = corners[side * wx, other * wy]
-    for side in range(2):
-        pack(edge_y.at[side], [corners[x, side * wy] for x in range(wx + 1)])
         pack(edge_x.at[side], [corners[side * wx, y] for y in range(wy + 1)])
-    for exchange in rims[1:-1]:
-        exchange.start()
+    rim[-1, 0].start()
+    rim[1, 0].start()
     final_y.start()
     final_x.start()
-    hear(3, -1, -1)
-    rims[0].start()
     hear(0, 1, 1)
-    rims[-1].start()
+    rim[1, 1].start()
 
     for c in range(columns):
         if c >= wy:

time: 17.1 us -> 17 us (level)
  no operation moved by 1% of the time
where the time goes in v8:
time: 17 us; the launch traced here: 16.9 us
  Pallas kernels  16.9 us (99%)
    pallas_call x1, Pallas kernels, local(): pl.pallas_call(functools.partial(kernel, count_x, count_y, wx, wy), out_s...  16 us
    pallas_call x1, Pallas kernels, local(): pl.pallas_call(functools.partial(deliver, faces, columns), out_shape=jax....  0.85 us

profile of v8, /device:TPU:409, one launch (start us, length us, event | category | flops | bytes accessed | tf_op | source)
XLA Modules:
  0.0 16.9 jit_solution(14344129284955874561)
XLA Ops:
  0.0 16.0 %apply.1.values = f32[3,884,128]{2,1,0:T(8,128)S(1)} custom-call(bf16[3,48,16,128]{3,2,1,0:T(8,128)(2,1)} %bitcast.6, s32[3,16,128]{2,1,0:T(8,128)} %bitcast.8, s32[16,128]{1,0:T(8,128)} %bitcast.9, f32[4]{0:T(128)} %viscosity_hbm.1, f32[16,128]{1,0:T(8,128)} %bitcast.10, bf16[288,256]{1,0:T(8,128)(2,1)} %bitcast.7, bf16[288,256]{1,0:T(8,128)(2,1)} %flux_hbm.1, ...), custom_call_target="tpu_custom_call" | custom-call | tf_op jit(solution)/shard_map/apply/pallas_call | solution.py:549
  16.0 0.9 %deliver.1 = bf16[3,48,16,128]{3,2,1,0:T(8,128)(2,1)} custom-call(f32[3,884,128]{2,1,0:T(8,128)S(1)} %apply.1.values), custom_call_target="tpu_custom_call" | custom-call | tf_op jit(solution)/shard_map/deliver/pallas_call | solution.py:558

commit v9 on v8

--- a/solution.py
+++ b/solution.py
@@ -379,16 +379,16 @@
     complete(1, rim_b)
     settle([place for place in vertices if place[1] >= wy - 1])
     pack_y(1)
+    rim[-1, 1].start()
+    hear(0, 1, 1)
+    rim[1, 1].start()
     rim[0, 1].start()
-    rim[-1, 1].start()
     for side in range(2):
         pack(edge_x.at[side], [corners[side * wx, y] for y in range(wy + 1)])
     rim[-1, 0].start()
     rim[1, 0].start()
     final_y.start()
     final_x.start()
-    hear(0, 1, 1)
-    rim[1, 1].start()
 
     for c in range(columns):
         if c >= wy:
@@ -469,9 +469,11 @@
         if side_x is not None and side_y is not None:
             value = value + rim_c[1 - side_x, 1 - side_y]
         fixes[x, y] = correct(value, present(int(x == wx), int(y == wy)))
-    final_x.arrive()
-    final_y.arrive()
+    outer.sort(key=lambda c: c in (wy - 1, (wx - 1) * wy))
     for start in range(0, len(outer), 4):
+        if start + 4 >= len(outer):
+            final_x.arrive()
+            final_y.arrive()
         emit(outer[start : start + 4])
 
 

time: 17 us -> 17.1 us (level)
  no operation moved by 1% of the time
where the time goes in v9:
time: 17.1 us; the launch traced here: 17 us
  Pallas kernels  17 us (99%)
    pallas_call x1, Pallas kernels, local(): pl.pallas_call(functools.partial(kernel, count_x, count_y, wx, wy), out_s...  16.1 us
    pallas_call x1, Pallas kernels, local(): pl.pallas_call(functools.partial(deliver, faces, columns), out_shape=jax....  0.85 us

profile of v9, /device:TPU:409, one launch (start us, length us, event | category | flops | bytes accessed | tf_op | source)
XLA Modules:
  0.0 17.0 jit_solution(3261111054550727752)
XLA Ops:
  0.0 16.1 %apply.1.values = f32[3,884,128]{2,1,0:T(8,128)S(1)} custom-call(bf16[3,48,16,128]{3,2,1,0:T(8,128)(2,1)} %bitcast.6, s32[3,16,128]{2,1,0:T(8,128)} %bitcast.8, s32[16,128]{1,0:T(8,128)} %bitcast.9, f32[4]{0:T(128)} %viscosity_hbm.1, f32[16,128]{1,0:T(8,128)} %bitcast.10, bf16[288,256]{1,0:T(8,128)(2,1)} %bitcast.7, bf16[288,256]{1,0:T(8,128)(2,1)} %flux_hbm.1, ...), custom_call_target="tpu_custom_call" | custom-call | tf_op jit(solution)/shard_map/apply/pallas_call | solution.py:551
  16.1 0.9 %deliver.1 = bf16[3,48,16,128]{3,2,1,0:T(8,128)(2,1)} custom-call(f32[3,884,128]{2,1,0:T(8,128)S(1)} %apply.1.values), custom_call_target="tpu_custom_call" | custom-call | tf_op jit(solution)/shard_map/deliver/pallas_call | solution.py:560
